TPU v7x, 32 devices: a whole 2x2x4 slice. The times are simulated.
32 devices in a mesh: band: 4 (over y, core), grid: 8 (over z, x).
Axes of the slice: x: 2, y: 2, z: 4, core: 2. Of those that a mesh axis runs over, the one named last changes fastest.
Arguments:
- wave: float32 [128, 64, 64, 128], P('grid', 'band'), may hold values from -1400 to 1400
- direction: float32 [128, 64, 64, 128], P('grid', 'band'), may hold values from -6 to 6
- potential: float32 [64, 64, 128], P('band', 'grid'), may hold values from -50 to 50
- rotation: float32 [384, 128], replicated, may hold values from -0.3125 to 0.3125
Outputs:
- new_block: float32 [128, 64, 64, 128], P(None, 'band', 'grid')
All inputs are finite; a program needn't handle non-finite values.
Results may differ from a plain program's by a relative error of at most 0.00016.
Values sent between devices are 32-bit elements; how exact they have to be, the bound alone decides.
No kernel may reach another device: no remote copies, remote signals or barrier semaphores. Data moves between devices by JAX's collectives and lax.ppermute only.
A program may use at most 704 MiB of HBM per device.

v0:
```python
import jax
import jax.numpy as jnp
from jax import lax
from jax.sharding import PartitionSpec as P

NX = 64
NY = 64
NZ = 128


STENCIL = (
    -5369.0 / 1800.0,
    12.0 / 7.0,
    -15.0 / 56.0,
    10.0 / 189.0,
    -1.0 / 112.0,
    2.0 / 1925.0,
    -1.0 / 16632.0,
)
LATTICE = 51.3


def with_halo(shard, sides, width):
    for axis, dim in sides:
        devices, length = (lax.axis_size(axis), shard.shape[dim])
        up = [(i, (i + 1) % devices) for i in range(devices)]
        down = [(j, i) for i, j in up]
        last = lax.slice_in_dim(shard, length - width, length, axis=dim)
        initial = lax.slice_in_dim(shard, 0, width, axis=dim)
        before = lax.ppermute(last, axis, up)
        after = lax.ppermute(initial, axis, down)
        shard = jnp.concatenate([before, shard, after], axis=dim)
    return shard


def axis_term(field, axis):
    total = STENCIL[0] * field
    for offset in range(1, 7):
        total = total + STENCIL[offset] * (
            jnp.roll(field, offset, axis) + jnp.roll(field, -offset, axis)
        )
    return total


def inner_products(stacked, ncells):
    high = lax.Precision.HIGHEST
    partial_sum = jnp.dot(stacked, stacked.T, precision=high) / ncells
    return lax.psum(partial_sum, ("band", "grid"))


def apply_basis(coefficients, stacked):
    return lax.dot_general(
        coefficients, stacked, (((0,), (0,)), ((), ())), precision=lax.Precision.HIGHEST
    )


def on_device(wave, direction, potential, rotation):
    local_pot = lax.all_gather(potential, "grid", axis=1, tiled=True)
    bands_here, planes, rows_y, depth = wave.shape
    total_x = planes * lax.axis_size("band")
    inverse_x = (total_x / LATTICE) ** 2
    inverse_y = (rows_y / LATTICE) ** 2
    inverse_z = (depth / LATTICE) ** 2
    padded = with_halo(wave, (("band", 1),), 6)
    along_x = STENCIL[0] * wave
    for offset in range(1, 7):
        along_x = along_x + STENCIL[offset] * (
            padded[:, 6 + offset : 6 + offset + planes]
            + padded[:, 6 - offset : 6 - offset + planes]
        )
    second = along_x * inverse_x + axis_term(wave, 2) * inverse_y + axis_term(wave, 3) * inverse_z
    hwave = -0.5 * second + local_pot[None] * wave
    ncells = NX * NY * NZ
    numer = jnp.sum(wave * hwave, axis=(1, 2, 3))
    denom = jnp.sum(wave * wave, axis=(1, 2, 3))
    numer, denom = lax.psum((numer, denom), "band")
    ritz = numer / denom
    resid = hwave - ritz[:, None, None, None] * wave
    rows_w, rows_r, rows_d = (
        lax.all_to_all(wave, "grid", split_axis=2, concat_axis=0, tiled=True),
        lax.all_to_all(resid, "grid", split_axis=2, concat_axis=0, tiled=True),
        lax.all_to_all(direction, "grid", split_axis=2, concat_axis=0, tiled=True),
    )
    total_bands = rows_w.shape[0]
    out_shape = rows_w.shape
    stacked = jnp.concatenate([rows_r, rows_w, rows_d], axis=0).reshape(3 * total_bands, -1)
    gram = inner_products(stacked, ncells)
    factor = jnp.linalg.cholesky(gram)
    solved = jax.scipy.linalg.solve_triangular(factor, rotation, lower=True, trans=1)
    mixed = apply_basis(solved, stacked)
    return mixed.reshape(out_shape)


def solution(mesh):
    return jax.shard_map(
        on_device,
        mesh=mesh,
        in_specs=(
            P("grid", "band", None, None),
            P("grid", "band", None, None),
            P("band", "grid", None),
            P(),
        ),
        out_specs=P(None, "band", "grid", None),
        check_vma=False,
    )
```

profile of v0, /device:TPU:0, one launch (start us, length us, event | category | flops | bytes accessed | tf_op | source)
XLA Modules:
  0.0 1144.1 jit_solution(8752095945358382932)
XLA Ops:
  6.5 14.2 %constant_dynamic-update-slice_fusion = (f32[16,22,64,128]{3,1,0,2:T(8,128)}, f32[16,16,64,128]{3,1,0,2:T(8,128)}) fusion(f32[16,16,64,128]{3,2,1,0:T(8,128)} %param.4), kind=kLoop, calls=%fused_computation.135 | loop fusion | bytes 25165824
  49.2 12.7 %fusion.103 = (f32[16,16,58,128]{3,1,0,2:T(8,128)}, f32[16,16,58,128]{3,1,0,2:T(8,128)}) fusion(f32[16,16,64,128]{3,1,0,2:T(8,128)} %get-tuple-element.30), kind=kLoop, calls=%fused_computation.159 | loop fusion | bytes 30408704 | tf_op jit(solution)/shard_map/jit(_roll_static)/slice | solution.py:40
  61.9 12.8 %fusion.101 = (f32[16,16,59,128]{3,1,0,2:T(8,128)}, f32[16,16,59,128]{3,1,0,2:T(8,128)}) fusion(f32[16,16,64,128]{3,1,0,2:T(8,128)} %get-tuple-element.30), kind=kLoop, calls=%fused_computation.157 | loop fusion | bytes 30932992 | tf_op jit(solution)/shard_map/jit(_roll_static)/slice | solution.py:40
  74.7 13.0 %fusion.99 = (f32[16,16,60,128]{3,1,0,2:T(8,128)}, f32[16,16,60,128]{3,1,0,2:T(8,128)}) fusion(f32[16,16,64,128]{3,1,0,2:T(8,128)} %get-tuple-element.30), kind=kLoop, calls=%fused_computation.155 | loop fusion | bytes 31457280 | tf_op jit(solution)/shard_map/jit(_roll_static)/slice | solution.py:40
  87.7 11.1 fusion.97
  98.8 11.6 %fusion.95 = (f32[16,16,62,128]{3,1,0,2:T(8,128)}, f32[16,16,62,128]{3,1,0,2:T(8,128)}) fusion(f32[16,16,64,128]{3,1,0,2:T(8,128)} %get-tuple-element.30), kind=kLoop, calls=%fused_computation.151 | loop fusion | bytes 32505856 | tf_op jit(solution)/shard_map/jit(_roll_static)/slice | solution.py:40
  183.1 28.1 %all-to-all-done.1 = f32[16,16,64,128]{3,1,0,2:T(8,128)} async-done(((f32[16,16,64,128]{3,1,0,2:T(8,128)}), f32[16,16,64,128]{3,1,0,2:T(8,128)}, u32[]{:S(2)}, u32[]{:S(2)}) %all-to-all-start.1) | async-done | bytes 8388640 | tf_op jit(solution)/shard_map/all_to_all | solution.py:80
  216.2 203.3 %all_gather.3 = f32[16,64,128]{2,1,0:T(8,128)S(1)} all-gather(f32[16,8,128]{2,1,0:T(8,128)S(1)} %copy-done.6), channel_id=1, replica_groups=mesh['band'=4,'grid'=8] {'grid'}, dimensions={1}, use_global_device_ids=true | all-gather | bytes 589824 | tf_op jit(solution)/shard_map/all_gather | solution.py:58
  425.7 13.0 %fusion.113 = (f32[16,16,64,123]{3,1,0,2:T(8,128)}, f32[16,16,64,123]{3,1,0,2:T(8,128)}) fusion(f32[16,16,64,128]{3,1,0,2:T(8,128)} %get-tuple-element.30), kind=kLoop, calls=%fused_computation.169 | loop fusion | bytes 32243712 | tf_op jit(solution)/shard_map/jit(_roll_static)/slice | solution.py:40
  465.4 149.7 %multiply_reduce_fusion.1 = (f32[16]{0:T(128)S(1)}, f32[16,16,64,128]{3,1,0,2:T(8,128)}) fusion(f32[16,16,64,128]{3,2,1,0:T(8,128)} %param.4, f32[16,16,64,128]{3,1,0,2:T(8,128)} %get-tuple-element.30, f32[16,64,128]{2,0,1:T(8,128)S(1)} %copy.146, f32[16,16,64,6]{3,1,0,2:T(8,128)} %get-tuple-element.76, f32[16,16,64,122]{3,1,0,2:T(8,128)} %get-tuple-element.78, ...), kind=kLoop, calls=%fused_computation.90 | loop fusion | flops 197132272 | bytes 280494144 | tf_op jit(solution)/shard_map/reduce_sum | solution.py:74
  620.8 14.0 %multiply_subtract_fusion = f32[16,16,64,128]{3,1,0,2:T(8,128)} fusion(f32[16,16,64,128]{3,1,0,2:T(8,128)} %get-tuple-element.24, f32[16]{0:T(128)S(1)} %div.17, f32[16,16,64,128]{3,2,1,0:T(8,128)} %param.4), kind=kLoop, calls=%fused_computation.88 | loop fusion | flops 4194304 | bytes 25165888 | tf_op jit(solution)/shard_map/sub | solution.py:78
  658.9 11.6 %copy.179 = f32[16,16,8,8,128]{4,3,1,0,2:T(8,128)} copy(f32[16,16,8,8,128]{4,1,0,3,2:T(8,128)} %bitcast.4) | data formatting | bytes 16777216 | tf_op jit(solution)/shard_map/all_to_all | solution.py:80
  680.0 11.6 %copy.178 = f32[16,16,8,8,128]{4,3,1,0,2:T(8,128)} copy(f32[16,16,8,8,128]{4,1,0,3,2:T(8,128)} %bitcast.8) | data formatting | bytes 16777216 | tf_op jit(solution)/shard_map/all_to_all | solution.py:82
  701.1 122.1 %all-to-all-done = f32[16,16,64,128]{3,1,0,2:T(8,128)} async-done(((f32[16,16,64,128]{3,1,0,2:T(8,128)}), f32[16,16,64,128]{3,1,0,2:T(8,128)}, u32[]{:S(2)}, u32[]{:S(2)}) %all-to-all-start) | async-done | bytes 8388640 | tf_op jit(solution)/shard_map/all_to_all | solution.py:81
  829.2 45.2 %fusion.61 = f32[384,384]{0,1:T(8,128)} fusion(f32[128,16,8,128]{3,0,2,1:T(8,128)} %bitcast.90, f32[128,16,8,128]{3,0,2,1:T(8,128)} %bitcast.89, f32[128,16,8,128]{3,0,2,1:T(8,128)S(1)} %bitcast.91), kind=kOutput, calls=%fused_computation.98 | convolution fusion | flops 29003759616 | bytes 25755648 | tf_op jit(solution)/shard_map/dot_general | solution.py:47
  874.5 11.6 %copy.180 = f32[16,16,8,8,128]{4,3,1,0,2:T(8,128)} copy(f32[16,16,8,8,128]{4,1,0,3,2:T(8,128)} %bitcast) | data formatting | bytes 16777216 | tf_op jit(solution)/shard_map/all_to_all | solution.py:81
  895.4 17.3 %maximum_bitcast_fusion = f32[16384,384]{0,1:T(8,128)} fusion(f32[128,16384]{1,0:T(8,128)} %concatenate.161, f32[128,16384]{1,0:T(8,128)} %concatenate.160, f32[128,16384]{1,0:T(8,128)} %concatenate.159), kind=kLoop, calls=%fused_computation.13 | loop fusion | flops 12582912 | bytes 50331648 | tf_op jit(solution)/shard_map/dot_general | solution.py:52
  912.7 25.1 %copy.160 = f32[16384,384]{1,0:T(8,128)} copy(f32[16384,384]{0,1:T(8,128)} %maximum_bitcast_fusion) | data formatting | bytes 50331648 | tf_op jit(solution)/shard_map/dot_general | solution.py:52
  937.8 63.1 %all-reduce.4.cloned.1.call-done = f32[384,384]{0,1:T(8,128)} async-done(((f32[384,384]{0,1:T(8,128)}), f32[384,384]{0,1:T(8,128)}) %all-reduce.4.cloned.1.call-update) | async-done | bytes 589840 | tf_op jit(solution)/shard_map/psum | solution.py:48
  1003.3 11.7 %cholesky.77 = f32[128,128]{1,0:T(8,128)S(1)} custom-call(f32[128,128]{1,0:T(8,128)S(1)} %cholesky.192), custom_call_target="Cholesky" | custom-call | tf_op jit(solution)/shard_map/jit(cholesky)/cholesky | solution.py:88
  1025.5 11.7 %cholesky.162 = f32[128,128]{1,0:T(8,128)S(1)} custom-call(f32[128,128]{1,0:T(8,128)S(1)} %cholesky.196), custom_call_target="Cholesky" | custom-call | tf_op jit(solution)/shard_map/jit(cholesky)/cholesky | solution.py:88
  1047.7 11.7 %cholesky.181 = f32[128,128]{1,0:T(8,128)S(1)} custom-call(f32[128,128]{1,0:T(8,128)S(1)} %convolution_subtract_fusion.3), custom_call_target="Cholesky" | custom-call | tf_op jit(solution)/shard_map/jit(cholesky)/cholesky | solution.py:88
  1068.5 29.5 %custom-call.25 = f32[3,128,128]{1,2,0:T(8,128)S(1)} custom-call(f32[3,128,128]{2,1,0:T(8,128)S(1)} %get-tuple-element.12), custom_call_target="InvertDiagBlocksLowerTriangular" | custom-call | tf_op jit(solution)/shard_map/jit(_solve_triangular)/triangular_solve | solution.py:89
  1099.3 29.4 %fusion.65 = f32[128,16,8,128]{3,0,2,1:T(8,128)S(1)} fusion(f32[16,8,128,384]{3,2,1,0:T(8,128)} %bitcast.85, f32[128,128]{1,0:T(8,128)S(1)} %fusion.77, f32[128,128]{1,0:T(8,128)S(1)} %fusion.79, f32[128,128]{1,0:T(8,128)S(1)} %fusion.80), kind=kOutput, calls=%fused_computation.104 | convolution fusion | flops 9663774720 | bytes 33751040 | tf_op jit(solution)/shard_map/dot_general | solution.py:52
  (107 shorter events, 248.9 us)
Async XLA Ops:
  20.7 190.4 %all-to-all-start.1 = ((f32[16,16,64,128]{3,1,0,2:T(8,128)}), f32[16,16,64,128]{3,1,0,2:T(8,128)}, u32[]{:S(2)}, u32[]{:S(2)}) async-start(f32[16,16,64,128]{3,1,0,2:T(8,128)} %get-tuple-element.30), calls=%async_computation.1 | async-start | bytes 16777216 | tf_op jit(solution)/shard_map/all_to_all | solution.py:80
  28.0 7.6 copy-start
  34.7 424.6 %collective-permute-start = (f32[16,6,64,128]{3,2,1,0:T(8,128)}, f32[16,6,64,128]{3,2,1,0:T(8,128)}, u32[]{:S(2)}, u32[]{:S(2)}) collective-permute-start(f32[16,6,64,128]{3,2,1,0:T(8,128)} %get-tuple-element.27), channel_id=1, source_target_pairs={{8,0},{16,8},{24,16},{0,24},{9,1},{17,9},{25,17},{1,25},{10,2},{18... | collective-permute-start | bytes 9437192 | tf_op jit(solution)/shard_map/ppermute | solution.py:31
  35.4 8.5 slice-start
  35.4 8.5 slice-start.1
  35.4 417.9 %collective-permute-start.1 = (f32[16,6,64,128]{3,2,1,0:T(8,128)}, f32[16,6,64,128]{3,2,1,0:T(8,128)}, u32[]{:S(2)}, u32[]{:S(2)}) collective-permute-start(f32[16,6,64,128]{3,2,1,0:T(8,128)} %get-tuple-element.28), channel_id=1, source_target_pairs={{0,8},{8,16},{16,24},{24,0},{1,9},{9,17},{17,25},{25,1},{2,10},{10... | collective-permute-start | bytes 9437192 | tf_op jit(solution)/shard_map/ppermute | solution.py:30
  87.7 22.7 %slice-start.2 = ((s8[8388608]{0:T(1024)(128)(4,1)}), s8[4194304]{0:T(1024)(128)(4,1)S(1)}, s32[]{:S(2)}) async-start(s8[8388608]{0:T(1024)(128)(4,1)} %bitcast.81), calls=%async_computation.6 | async-start | bytes 8388608
  98.8 11.6 %slice-start.3 = ((s8[8388608]{0:T(1024)(128)(4,1)}), s8[4194304]{0:T(1024)(128)(4,1)S(1)}, s32[]{:S(2)}) async-start(s8[8388608]{0:T(1024)(128)(4,1)} %bitcast.81), calls=%async_computation.7 | async-start | bytes 8388608
  183.1 33.1 %copy-start.6 = (f32[16,8,128]{2,1,0:T(8,128)S(1)}, f32[16,8,128]{2,1,0:T(8,128)}, u32[]{:S(2)}) copy-start(f32[16,8,128]{2,1,0:T(8,128)} %param.6) | copy-start | bytes 196612
  211.1 423.6 %all-to-all-start.2 = ((f32[16,16,64,128]{3,1,0,2:T(8,128)}), f32[16,16,64,128]{3,1,0,2:T(8,128)}, u32[]{:S(2)}, u32[]{:S(2)}) async-start(f32[16,16,64,128]{3,1,0,2:T(8,128)} %copy.155), calls=%async_computation.2 | async-start | bytes 16777216 | tf_op jit(solution)/shard_map/all_to_all | solution.py:82
  421.4 17.2 %slice-start.4 = ((s8[8388608]{0:T(1024)(128)(4,1)}), s8[4194304]{0:T(1024)(128)(4,1)S(1)}, s32[]{:S(2)}) async-start(s8[8388608]{0:T(1024)(128)(4,1)} %bitcast.83), calls=%async_computation.8 | async-start | bytes 8388608
  425.7 13.0 %slice-start.5 = ((s8[8388608]{0:T(1024)(128)(4,1)}), s8[4194304]{0:T(1024)(128)(4,1)S(1)}, s32[]{:S(2)}) async-start(s8[8388608]{0:T(1024)(128)(4,1)} %bitcast.83), calls=%async_computation.9 | async-start | bytes 8388608
  453.3 12.0 %copy-start.1 = (f32[16,16,6,128]{3,1,0,2:T(8,128)S(1)}, f32[16,16,6,128]{3,1,0,2:T(8,128)}, u32[]{:S(2)}) copy-start(f32[16,16,6,128]{3,1,0,2:T(8,128)} %get-tuple-element.51) | copy-start | bytes 2359300
  453.3 12.0 %copy-start.2 = (f32[16,16,6,128]{3,1,0,2:T(8,128)S(1)}, f32[16,16,6,128]{3,1,0,2:T(8,128)}, u32[]{:S(2)}) copy-start(f32[16,16,6,128]{3,1,0,2:T(8,128)} %get-tuple-element.52) | copy-start | bytes 2359300
  453.3 12.0 %copy-start.3 = (f32[16,16,5,128]{3,1,0,2:T(8,128)S(1)}, f32[16,16,5,128]{3,1,0,2:T(8,128)}, u32[]{:S(2)}) copy-start(f32[16,16,5,128]{3,1,0,2:T(8,128)} %get-tuple-element.47) | copy-start | bytes 1966084
  453.3 12.0 %copy-start.4 = (f32[16,16,5,128]{3,1,0,2:T(8,128)S(1)}, f32[16,16,5,128]{3,1,0,2:T(8,128)}, u32[]{:S(2)}) copy-start(f32[16,16,5,128]{3,1,0,2:T(8,128)} %get-tuple-element.48) | copy-start | bytes 1966084
  634.8 188.4 %all-to-all-start = ((f32[16,16,64,128]{3,1,0,2:T(8,128)}), f32[16,16,64,128]{3,1,0,2:T(8,128)}, u32[]{:S(2)}, u32[]{:S(2)}) async-start(f32[16,16,64,128]{3,1,0,2:T(8,128)} %multiply_subtract_fusion), calls=%async_computation | async-start | bytes 16777216 | tf_op jit(solution)/shard_map/all_to_all | solution.py:81
  639.8 361.1 %all-reduce.4.cloned.1.call-start = ((), (), s32[]{:S(2)}) async-start(), calls=%async_computation.3 | async-start | bytes 1179648 | tf_op jit(solution)/shard_map/psum | solution.py:48
  912.7 185.3 %copy-start.5 = (f32[384,128]{1,0:T(8,128)S(1)}, f32[384,128]{1,0:T(8,128)}, u32[]{:S(2)}) copy-start(f32[384,128]{1,0:T(8,128)} %param.7) | copy-start | bytes 589828
Sparse Core Ops, SparseCore 0:
  874.6 126.2 all-reduce.3
where the time goes:
time: 1150 us; the launch traced here: 1140 us
  local copies, waits for them, and re-layouts  338 us (29%)
  other arithmetic  272 us (24%)
  waiting for transfers between devices  213 us (19%)
  blocking collectives  209 us (18%)
  matrix products  76.9 us (7%)
  starting transfers between devices  18.6 us (2%)
  between operations  15.8 us (1%)
    all_gather x1, blocking collectives, on_device(): local_pot = lax.all_gather(potential, 'grid', axis=1, tiled=True)  203 us
    slice x24, local copies, waits for them, and re-layouts, axis_term(): jnp.roll(field, offset, axis) + jnp.roll(field, -offset, axis)  168 us
    reduce_sum x1, other arithmetic, on_device(): numer = jnp.sum(wave * hwave, axis=(1, 2, 3))  150 us
    all_to_all x1, waiting for transfers between devices, on_device(): lax.all_to_all(resid, 'grid', split_axis=2, concat_axis=0, tiled=True)  122 us
    psum x1, waiting for transfers between devices, inner_products(): return lax.psum(partial_sum, ('band', 'grid'))  63.1 us
    another operation x10, other arithmetic, on_device(): factor = jnp.linalg.cholesky(gram)  56.3 us
    dot_general x1, matrix products, inner_products(): partial_sum = jnp.dot(stacked, stacked.T, precision=high) / ncells  45.2 us
    dot_general x2, local copies, waits for them, and re-layouts, apply_basis(): lax.dot_general(coefficients, stacked, (((0,), (0,)), ((), ())), precisio...  33.4 us
  transfers between devices with their start and end apart: 6, of which 3 were waited for; matrix products, arithmetic and copies ran while one was open for 43% of the time, Pallas kernels for 0%

commit v1 on v0

v1 whole, which is shorter than its diff:
```python
import functools

import jax
import jax.numpy as jnp
from jax import lax
from jax.experimental import pallas as pl
from jax.experimental.pallas import tpu as pltpu
from jax.sharding import PartitionSpec as P

STENCIL = (
    -5369.0 / 1800.0,
    12.0 / 7.0,
    -15.0 / 56.0,
    10.0 / 189.0,
    -1.0 / 112.0,
    2.0 / 1925.0,
    -1.0 / 16632.0,
)
LATTICE = 51.3
WIDTH = len(STENCIL) - 1
HIGH = lax.Precision.HIGHEST
F32 = jnp.float32
BF16 = jnp.bfloat16


def halos(shard, axis, dim):
    devices, length = lax.axis_size(axis), shard.shape[dim]
    up = [(i, (i + 1) % devices) for i in range(devices)]
    down = [(j, i) for i, j in up]
    last = lax.slice_in_dim(shard, length - WIDTH, length, axis=dim)
    first = lax.slice_in_dim(shard, 0, WIDTH, axis=dim)
    return lax.ppermute(last, axis, up), lax.ppermute(first, axis, down)


def butterfly_sum(value):
    for axis in ("band", "grid"):
        devices, step = lax.axis_size(axis), 1
        while step < devices:
            value = value + lax.ppermute(
                value, axis, [(i, i ^ step) for i in range(devices)]
            )
            step *= 2
    return value


def kinetic_kernel(weights, w_ref, lo_ref, hi_ref, t_ref, s_ref, pad):
    _, planes, rows, depth = w_ref.shape
    parts, _, _, mine, _ = t_ref.shape
    center, along_x, along_y, along_z = weights
    pad[0:WIDTH] = lo_ref[0]
    pad[WIDTH : WIDTH + planes] = w_ref[0]
    pad[WIDTH + planes :] = hi_ref[0]

    def plane(i, total):
        here = pad[i + WIDTH]
        out = center * here
        for k in range(1, WIDTH + 1):
            out += along_x[k - 1] * (pad[i + WIDTH + k] + pad[i + WIDTH - k])
            out += along_y[k - 1] * (
                pltpu.roll(here, k, 0) + pltpu.roll(here, rows - k, 0)
            )
            out += along_z[k - 1] * (
                pltpu.roll(here, k, 1) + pltpu.roll(here, depth - k, 1)
            )
        t_ref[:, 0, i] = out.reshape(parts, mine, depth)
        return total + (here * out).reshape(-1, 8, depth).sum(0)

    s_ref[0] = lax.fori_loop(0, planes, plane, jnp.zeros((8, depth), F32))


def kinetic(wave, before, after, weights, parts):
    bands, planes, rows, depth = wave.shape
    spec = lambda n: pl.BlockSpec((1, n, rows, depth), lambda b: (b, 0, 0, 0))
    return pl.pallas_call(
        functools.partial(kinetic_kernel, weights),
        grid=(bands,),
        in_specs=[spec(planes), spec(WIDTH), spec(WIDTH)],
        out_specs=[
            pl.BlockSpec(
                (parts, 1, planes, rows // parts, depth), lambda b: (0, b, 0, 0, 0)
            ),
            pl.BlockSpec((1, 8, depth), lambda b: (b, 0, 0)),
        ],
        out_shape=[
            jax.ShapeDtypeStruct((parts, bands, planes, rows // parts, depth), F32),
            jax.ShapeDtypeStruct((bands, 8, depth), F32),
        ],
        scratch_shapes=[pltpu.VMEM((planes + 2 * WIDTH, rows, depth), F32)],
        compiler_params=pltpu.CompilerParams(vmem_limit_bytes=32 << 20),
        cost_estimate=pl.CostEstimate(
            flops=60 * wave.size, bytes_accessed=11 * wave.size, transcendentals=0
        ),
        name="kinetic",
    )(wave, before, after)


def split(value):
    high = value.astype(BF16)
    return high, (value - high.astype(F32)).astype(BF16)


def dot_t(a, b, precision=None):
    return lax.dot_general(
        a, b, (((1,), (1,)), ((), ())), precision=precision, preferred_element_type=F32
    )


def dot(a, b, precision=None):
    return jnp.dot(a, b, precision=precision, preferred_element_type=F32)


def row_of(ref, i):
    bands, planes, mine, depth = ref.shape
    flat = ref.reshape(bands * planes * mine, depth)
    return flat[pl.ds(i, bands, stride=planes * mine), :]


def split_rows(ref):
    count = ref.shape[1] * ref.shape[2]
    highs, lows = zip(*(split(row_of(ref, i)) for i in range(count)))
    return jnp.concatenate(highs, axis=1), jnp.concatenate(lows, axis=1)


def gram_pair_kernel(t_ref, w_ref, v_ref, ritz_ref, g_ref, high_ref, low_ref, acc, cross):
    step, last = pl.program_id(0), pl.num_programs(0) - 1
    _, planes, mine, depth = w_ref.shape

    @pl.when(step == 0)
    def _():
        acc[...] = jnp.zeros_like(acc)
        cross[...] = jnp.zeros_like(cross)

    for i in range(planes * mine):
        w = row_of(w_ref, i)
        x, y = i // mine, i % mine
        r = row_of(t_ref, i) + (v_ref[x, y : y + 1, :] - ritz_ref[...]) * w
        high, low = split(jnp.concatenate([r, w], axis=0))
        high_ref[:, i * depth : (i + 1) * depth] = high
        low_ref[:, i * depth : (i + 1) * depth] = low
    high = high_ref[...]
    acc[...] += dot_t(high, high)
    cross[...] += dot_t(high, low_ref[...])

    @pl.when(step == last)
    def _():
        g_ref[...] = acc[...] + (cross[...] + cross[...].T)


def gram_row_kernel(high_ref, low_ref, d_ref, g_ref, acc):
    step, last = pl.program_id(0), pl.num_programs(0) - 1
    bands = d_ref.shape[0]

    @pl.when(step == 0)
    def _():
        acc[...] = jnp.zeros_like(acc)

    high, low = split_rows(d_ref)
    both = jnp.concatenate([high, low], axis=0)
    wide = dot_t(jnp.concatenate([high_ref[...], high], axis=0), both)
    acc[...] += wide[:, :bands] + wide[:, bands:]
    rest = dot_t(jnp.concatenate([low_ref[...], low], axis=0), high)
    acc[...] += rest

    @pl.when(step == last)
    def _():
        g_ref[...] = acc[...].T


def apply_kernel(high_ref, low_ref, d_ref, c_ref, o_ref):
    bands, planes, mine, depth = o_ref.shape
    d_high, d_low = split_rows(d_ref)
    c_high, c_low = split(c_ref[...])
    wide = dot(
        jnp.concatenate([c_high, c_low], axis=0),
        jnp.concatenate([high_ref[...], d_high], axis=0),
    )
    out = wide[:bands] + wide[bands:]
    out += dot(c_high, jnp.concatenate([low_ref[...], d_low], axis=0))
    flat = o_ref.reshape(bands * planes * mine, depth)
    for i in range(planes * mine):
        flat[pl.ds(i, bands, stride=planes * mine), :] = out[:, i * depth : (i + 1) * depth]


def tile_spec(bands, planes, mine, depth):
    return pl.BlockSpec((bands, planes, mine, depth), lambda x: (0, x, 0, 0))


def cost(flops, nbytes):
    return pl.CostEstimate(flops=flops, bytes_accessed=nbytes, transcendentals=0)


STEP = 2


def gram_pair(t, w, v, ritz):
    bands, planes, mine, depth = w.shape
    tile = tile_spec(bands, STEP, mine, depth)
    points = pl.BlockSpec((2 * bands, STEP * mine * depth), lambda x: (0, x))
    parts = jax.ShapeDtypeStruct((2 * bands, planes * mine * depth), BF16)
    square = (2 * bands, 2 * bands)
    return pl.pallas_call(
        gram_pair_kernel,
        grid=(planes // STEP,),
        in_specs=[
            tile,
            tile,
            pl.BlockSpec((STEP, mine, depth), lambda x: (x, 0, 0)),
            pl.BlockSpec((bands, depth), lambda x: (0, 0)),
        ],
        out_specs=[pl.BlockSpec(square, lambda x: (0, 0)), points, points],
        out_shape=[jax.ShapeDtypeStruct(square, F32), parts, parts],
        scratch_shapes=[pltpu.VMEM(square, F32), pltpu.VMEM(square, F32)],
        compiler_params=pltpu.CompilerParams(vmem_limit_bytes=40 << 20),
        cost_estimate=cost(16 * bands * w.size, 16 * w.size),
        name="gram_pair",
    )(t, w, v, ritz)


def gram_row(high, low, d):
    bands, planes, mine, depth = d.shape
    points = pl.BlockSpec((2 * bands, STEP * mine * depth), lambda x: (0, x))
    return pl.pallas_call(
        gram_row_kernel,
        grid=(planes // STEP,),
        in_specs=[points, points, tile_spec(bands, STEP, mine, depth)],
        out_specs=pl.BlockSpec((bands, 3 * bands), lambda x: (0, 0)),
        out_shape=jax.ShapeDtypeStruct((bands, 3 * bands), F32),
        scratch_shapes=[pltpu.VMEM((3 * bands, bands), F32)],
        compiler_params=pltpu.CompilerParams(vmem_limit_bytes=40 << 20),
        cost_estimate=cost(18 * bands * d.size, 12 * d.size),
        name="gram_row",
    )(high, low, d)


def apply_basis(high, low, d, coefficients):
    bands, planes, mine, depth = d.shape
    points = pl.BlockSpec((2 * bands, STEP * mine * depth), lambda x: (0, x))
    tile = tile_spec(bands, STEP, mine, depth)
    return pl.pallas_call(
        apply_kernel,
        grid=(planes // STEP,),
        in_specs=[points, points, tile, pl.BlockSpec((bands, 3 * bands), lambda x: (0, 0))],
        out_specs=tile,
        out_shape=jax.ShapeDtypeStruct(d.shape, F32),
        compiler_params=pltpu.CompilerParams(vmem_limit_bytes=40 << 20),
        cost_estimate=cost(18 * bands * d.size, 16 * d.size),
        name="apply_basis",
    )(high, low, d, coefficients)


def spread_row(value, i):
    return jnp.broadcast_to(value[i : i + 1, :], value.shape)


def spread_column(value, j):
    return jnp.broadcast_to(value[:, j : j + 1], value.shape)


def inverse_factor(matrix):
    size = matrix.shape[0]
    count = size // 8
    shape = (8, size)
    sublane = lax.broadcasted_iota(jnp.int32, shape, 0)
    lane = lax.broadcasted_iota(jnp.int32, shape, 1)
    left = [matrix[8 * q : 8 * q + 8] for q in range(count)]
    right = [jnp.where(lane == sublane + 8 * q, 1.0, 0.0).astype(F32) for q in range(count)]
    done = []
    for p in range(count):
        base = 8 * p
        rows = [spread_row(left[p], i) for i in range(8)]
        ones = [spread_row(right[p], i) for i in range(8)]
        entry = {
            (i, j): spread_column(rows[i], base + j) for i in range(8) for j in range(i, 8)
        }
        unit, inverse = {}, []
        for k in range(8):
            inverse.append(1.0 / entry[k, k])
            for i in range(k + 1, 8):
                unit[i, k] = entry[k, i] * inverse[k]
            for i in range(k + 1, 8):
                for j in range(i, 8):
                    entry[i, j] = entry[i, j] - unit[i, k] * entry[k, j]
        for i in range(8):
            for k in range(i):
                rows[i] = rows[i] - unit[i, k] * rows[k]
                ones[i] = ones[i] - unit[i, k] * ones[k]
        out = ones[0] * lax.rsqrt(entry[0, 0])
        for i in range(1, 8):
            out = jnp.where(sublane == i, ones[i] * lax.rsqrt(entry[i, i]), out)
        done.append(out)
        if p == count - 1:
            break
        for i in reversed(range(8)):
            rows[i] = rows[i] * inverse[i]
            ones[i] = ones[i] * inverse[i]
            for k in range(i + 1, 8):
                rows[i] = rows[i] - unit[k, i] * rows[k]
                ones[i] = ones[i] - unit[k, i] * ones[k]
        for q in range(p + 1, count):
            columns = [spread_column(left[q], base + i) for i in range(8)]
            for i in range(8):
                left[q] = left[q] - columns[i] * rows[i]
                right[q] = right[q] - columns[i] * ones[i]
    return jnp.concatenate(done, axis=0)


def factor_pair_kernel(scale, g_ref, o_ref):
    half = g_ref.shape[0] // 2
    first = inverse_factor(g_ref[:half, :half] * scale)
    lower = dot_t(g_ref[half:, :half] * scale, first, HIGH)
    second = inverse_factor(g_ref[half:, half:] * scale - dot_t(lower, lower, HIGH))
    o_ref[:half, :half] = first
    o_ref[:half, half:] = jnp.zeros((half, half), F32)
    o_ref[half:, :half] = -dot(second, dot(lower, first, HIGH), HIGH)
    o_ref[half:, half:] = second


def factor_pair(gram, scale):
    return pl.pallas_call(
        functools.partial(factor_pair_kernel, scale),
        out_shape=jax.ShapeDtypeStruct(gram.shape, F32),
        cost_estimate=cost(10**8, 4 * gram.size),
        name="factor_pair",
    )(gram)


def coefficients_kernel(scale, row_ref, pair_ref, turned_ref, o_ref):
    bands = row_ref.shape[0]
    pair = pair_ref[...]
    lower = dot_t(row_ref[:, : 2 * bands] * scale, pair, HIGH)
    last = inverse_factor(row_ref[:, 2 * bands :] * scale - dot_t(lower, lower, HIGH))
    tail = dot(turned_ref[:, 2 * bands :], last, HIGH)
    o_ref[:, 2 * bands :] = tail
    o_ref[:, : 2 * bands] = dot(turned_ref[:, : 2 * bands] - dot(tail, lower, HIGH), pair, HIGH)


def coefficients_of(row, pair, turned, scale):
    return pl.pallas_call(
        functools.partial(coefficients_kernel, scale),
        out_shape=jax.ShapeDtypeStruct(row.shape, F32),
        cost_estimate=cost(10**8, 4 * row.size),
        name="coefficients",
    )(row, pair, turned)


def fast(wave, direction, potential, rotation):
    bands_here, planes, rows_y, depth = wave.shape
    parts = lax.axis_size("grid")
    bands, mine = bands_here * parts, rows_y // parts
    total_x = planes * lax.axis_size("band")
    scale = [-0.5 * (n / LATTICE) ** 2 for n in (total_x, rows_y, depth)]
    weights = (
        STENCIL[0] * sum(scale),
        *([s * c for c in STENCIL[1:]] for s in scale),
    )
    ncells = total_x * rows_y * depth

    def pack(field):
        cut = field.reshape(bands_here, planes, parts, mine, depth)
        return cut.transpose(2, 0, 1, 3, 4)

    def exchange(blocks):
        got = lax.all_to_all(blocks, "grid", 0, 0, tiled=True)
        return got.reshape(bands, planes, mine, depth)

    before, after = halos(wave, "band", 1)
    w = exchange(pack(wave))
    sent, own = kinetic(wave, before, after, weights, parts)
    own = lax.dynamic_update_slice(
        jnp.zeros((bands,), F32),
        own.sum((1, 2)),
        (lax.axis_index("grid") * bands_here,),
    )
    square = w * w
    numer = own + jnp.sum(square * potential[None], axis=(1, 2, 3))
    sums = butterfly_sum(jnp.stack([numer, jnp.sum(square, axis=(1, 2, 3))]))
    t = exchange(sent)
    d_sent, sums = lax.optimization_barrier((pack(direction), sums))
    ritz = jnp.broadcast_to((sums[0] / sums[1])[:, None], (bands, depth))
    d = exchange(d_sent)

    pair, high, low = gram_pair(t, w, potential, ritz)
    pair = butterfly_sum(pair)
    row = gram_row(high, low, d)
    inverse = factor_pair(pair, 1.0 / ncells)
    row = butterfly_sum(row)
    solved = coefficients_of(row, inverse, rotation.T, 1.0 / ncells)
    return apply_basis(high, low, d, solved)


def axis_term(field, axis):
    total = STENCIL[0] * field
    for k in range(1, WIDTH + 1):
        total = total + STENCIL[k] * (jnp.roll(field, k, axis) + jnp.roll(field, -k, axis))
    return total


def general(wave, direction, potential, rotation):
    bands_here, planes, rows_y, depth = wave.shape
    total_x = planes * lax.axis_size("band")
    inverse_x, inverse_y, inverse_z = ((n / LATTICE) ** 2 for n in (total_x, rows_y, depth))
    before, after = halos(wave, "band", 1)
    padded = jnp.concatenate([before, wave, after], axis=1)
    along_x = STENCIL[0] * wave
    for k in range(1, WIDTH + 1):
        along_x = along_x + STENCIL[k] * (
            padded[:, WIDTH + k : WIDTH + k + planes]
            + padded[:, WIDTH - k : WIDTH - k + planes]
        )
    second = along_x * inverse_x + axis_term(wave, 2) * inverse_y + axis_term(wave, 3) * inverse_z
    local_pot = lax.all_gather(potential, "grid", axis=1, tiled=True)
    hwave = -0.5 * second + local_pot[None] * wave
    numer = jnp.sum(wave * hwave, axis=(1, 2, 3))
    denom = jnp.sum(wave * wave, axis=(1, 2, 3))
    numer, denom = lax.psum((numer, denom), "band")
    resid = hwave - (numer / denom)[:, None, None, None] * wave
    gathered = [
        lax.all_to_all(f, "grid", split_axis=2, concat_axis=0, tiled=True)
        for f in (resid, wave, direction)
    ]
    out_shape = gathered[0].shape
    stacked = jnp.concatenate(gathered, axis=0).reshape(3 * out_shape[0], -1)
    ncells = total_x * rows_y * depth
    gram = lax.psum(jnp.dot(stacked, stacked.T, precision=HIGH) / ncells, ("band", "grid"))
    factor = jnp.linalg.cholesky(gram)
    solved = jax.scipy.linalg.solve_triangular(factor, rotation, lower=True, trans=1)
    mixed = lax.dot_general(solved, stacked, (((0,), (0,)), ((), ())), precision=HIGH)
    return mixed.reshape(out_shape)


def on_device(wave, direction, potential, rotation):
    _, planes, rows_y, depth = wave.shape
    mine = rows_y // lax.axis_size("grid")
    tiled = mine == 8 and depth == 128 and planes % STEP == 0
    return (fast if tiled else general)(wave, direction, potential, rotation)


def solution(mesh):
    return jax.shard_map(
        on_device,
        mesh=mesh,
        in_specs=(
            P("grid", "band", None, None),
            P("grid", "band", None, None),
            P("band", "grid", None),
            P(),
        ),
        out_specs=P(None, "band", "grid", None),
        check_vma=False,
    )
```

time: 1150 us -> 672 us (0.58)
  local copies, waits for them, and re-layouts: 338 us -> 35.2 us
  other arithmetic: 272 us -> 7.02 us
  waiting for transfers between devices: 213 us -> 476 us
  blocking collectives: 209 us -> 0 us
  Pallas kernels: 0 us -> 117 us
  matrix products: 76.9 us -> 0 us
  starting transfers between devices: 18.6 us -> 35.3 us
  between operations: 15.8 us -> 0.21 us
    ppermute x2 -> x17, waiting for transfers between devices: 0.01 us -> 259 us  [the longest x15 191 us: butterfly_sum(): lax.ppermute(value, axis, [(i, i ^ step) for i in range(devices)])]
    all_gather x1 -> x0, blocking collectives: 203 us -> none  [on_device(): local_pot = lax.all_gather(potential, 'grid', axis=1, tiled=True)]
    slice x25 -> x1, local copies, waits for them, and re-layouts: 175 us -> 3.96 us  [halos(): first = lax.slice_in_dim(shard, 0, WIDTH, axis=dim)]
    reduce_sum x2, other arithmetic: 154 us -> 5.26 us  [the longest x1 5.06 us: fast(): numer = own + jnp.sum(square * potential[None], axis=(1, 2, 3))]
    pallas_call x0 -> x6, Pallas kernels: none -> 117 us  [the longest x1 48.1 us: kinetic(): pl.pallas_call(functools.partial(kinetic_kernel, weights), grid=(bands,),...]
    another operation x13 -> x2, other arithmetic: 85.9 us -> 0.08 us  [fast(): sums = butterfly_sum(jnp.stack([numer, jnp.sum(square, axis=(1, 2, 3))]))]
    dot_general x2 -> x0, matrix products: 74.6 us -> none  [the longest x1 45.2 us: inner_products(): partial_sum = jnp.dot(stacked, stacked.T, precision=high) / ncells]
    all_to_all x3, waiting for transfers between devices: 150 us -> 217 us  [exchange(): got = lax.all_to_all(blocks, 'grid', 0, 0, tiled=True)]
  transfers between devices with their start and end apart: 6 -> 20, of which waited for: 3 -> 15; matrix products, arithmetic and copies ran while one was open for 43% -> 3% of each run, Pallas kernels for 0% -> 14%
where the time goes in v1:
time: 672 us; the launch traced here: 671 us
  waiting for transfers between devices  476 us (71%)
  Pallas kernels  117 us (17%)
  starting transfers between devices  35.3 us (5%)
  local copies, waits for them, and re-layouts  35.2 us (5%)
  other arithmetic  7.02 us (1%)
    all_to_all x3, waiting for transfers between devices, exchange(): got = lax.all_to_all(blocks, 'grid', 0, 0, tiled=True)  217 us
    ppermute x15, waiting for transfers between devices, butterfly_sum(): lax.ppermute(value, axis, [(i, i ^ step) for i in range(devices)])  191 us
    ppermute x2, waiting for transfers between devices, halos(): return (lax.ppermute(last, axis, up), lax.ppermute(first, axis, down))  67.7 us
    pallas_call x1, Pallas kernels, kinetic(): pl.pallas_call(functools.partial(kinetic_kernel, weights), grid=(bands,),...  48.1 us
    all_to_all x3, starting transfers between devices, exchange(): got = lax.all_to_all(blocks, 'grid', 0, 0, tiled=True)  17.4 us
    pallas_call x1, Pallas kernels, gram_pair(): pl.pallas_call(gram_pair_kernel, grid=(planes // STEP,), in_specs=[tile,...  16.4 us
    ppermute x15, starting transfers between devices, butterfly_sum(): lax.ppermute(value, axis, [(i, i ^ step) for i in range(devices)])  16 us
    transpose x2, local copies, waits for them, and re-layouts, pack(): return cut.transpose(2, 0, 1, 3, 4)  15.6 us
  transfers between devices with their start and end apart: 20, of which 15 were waited for; matrix products, arithmetic and copies ran while one was open for 3% of the time, Pallas kernels for 14%

profile of v1, /device:TPU:0, one launch (start us, length us, event | category | flops | bytes accessed | tf_op | source)
XLA Modules:
  0.0 670.6 jit_solution(7251638333624278259)
XLA Ops:
  0.0 7.8 %copy_bitcast_fusion.1 = f32[8,16,16,8,128]{4,3,2,1,0:T(8,128)} fusion(f32[16,16,64,128]{3,2,1,0:T(8,128)} %w_ref.1), kind=kLoop, calls=%fused_computation.1 | loop fusion | bytes 16777216 | tf_op jit(solution)/shard_map/transpose | solution.py:360
  7.8 7.3 %all-to-all-start.1 = ((f32[8,16,16,8,128]{4,3,2,1,0:T(8,128)}), f32[8,16,16,8,128]{4,3,2,1,0:T(8,128)}, u32[]{:S(2)}, u32[]{:S(2)}) async-start(f32[8,16,16,8,128]{4,3,2,1,0:T(8,128)} %copy_bitcast_fusion.1), calls=%async_computation.1 | async-start | bytes 16777216 | tf_op jit(solution)/shard_map/all_to_all | solution.py:363
  15.1 4.0 fusion.2
  20.8 66.8 %collective-permute-done.lo_ref = f32[16,6,64,128]{3,2,1,0:T(8,128)S(1)} collective-permute-done((f32[16,6,64,128]{3,2,1,0:T(8,128)S(1)}, f32[16,6,64,128]{3,2,1,0:T(8,128)S(1)}, u32[]{:S(2)}, u32[]{:S(2)}) %collective-permute-start) | collective-permute-done | bytes 3145760 | tf_op jit(solution)/shard_map/ppermute | solution.py:32
  88.5 48.1 %kinetic.1 = (f32[8,16,16,8,128]{4,3,2,1,0:T(8,128)S(1)}, f32[16,8,128]{2,1,0:T(8,128)S(1)}) custom-call(f32[16,16,64,128]{3,2,1,0:T(8,128)} %w_ref.1, f32[16,6,64,128]{3,2,1,0:T(8,128)S(1)} %collective-permute-done.lo_ref, f32[16,6,64,128]{3,2,1,0:T(8,128)S(1)} %collective-permute-done.1.hi_ref), custom_call_target="tpu_custom_call" | custom-call | flops 125829120 | bytes 23068672 | tf_op jit(solution)/shard_map/kinetic/pallas_call | solution.py:74
  140.0 58.2 %all-to-all-done.1 = f32[8,16,16,8,128]{4,3,2,1,0:T(8,128)} async-done(((f32[8,16,16,8,128]{4,3,2,1,0:T(8,128)}), f32[8,16,16,8,128]{4,3,2,1,0:T(8,128)}, u32[]{:S(2)}, u32[]{:S(2)}) %all-to-all-start.1) | async-done | bytes 8388640 | tf_op jit(solution)/shard_map/all_to_all | solution.py:363
  198.2 5.2 all-to-all-start
  203.6 5.1 multiply_reduce_fusion
  216.0 54.3 %collective-permute-done.4 = f32[2,128]{1,0:T(2,128)S(1)} collective-permute-done((f32[2,128]{1,0:T(2,128)S(1)}, f32[2,128]{1,0:T(2,128)S(1)}, u32[]{:S(2)}, u32[]{:S(2)}) %collective-permute-start.4) | collective-permute-done | bytes 1056 | tf_op jit(solution)/shard_map/ppermute | solution.py:39
  271.9 66.4 %collective-permute-done.5 = f32[2,128]{1,0:T(2,128)S(1)} collective-permute-done((f32[2,128]{1,0:T(2,128)S(1)}, f32[2,128]{1,0:T(2,128)S(1)}, u32[]{:S(2)}, u32[]{:S(2)}) %collective-permute-start.5) | collective-permute-done | bytes 1056 | tf_op jit(solution)/shard_map/ppermute | solution.py:39
  338.3 3.9 collective-permute-start.6
  342.2 7.8 %copy_bitcast_fusion = f32[8,16,16,8,128]{4,3,2,1,0:T(8,128)} fusion(f32[16,16,64,128]{3,2,1,0:T(8,128)} %param.5), kind=kLoop, calls=%fused_computation | loop fusion | bytes 16777216 | tf_op jit(solution)/shard_map/transpose | solution.py:360
  350.0 35.7 %collective-permute-done.6 = f32[2,128]{1,0:T(2,128)S(1)} collective-permute-done((f32[2,128]{1,0:T(2,128)S(1)}, f32[2,128]{1,0:T(2,128)S(1)}, u32[]{:S(2)}, u32[]{:S(2)}) %collective-permute-start.6) | collective-permute-done | bytes 1056 | tf_op jit(solution)/shard_map/ppermute | solution.py:39
  385.7 5.0 all-to-all-start.2
  390.7 16.4 %gram_pair.1 = (f32[256,256]{1,0:T(8,128)S(1)}, bf16[256,16384]{1,0:T(8,128)(2,1)S(1)}, bf16[256,16384]{1,0:T(8,128)(2,1)}) custom-call(f32[128,16,8,128]{3,2,1,0:T(8,128)} %bitcast.t_ref, f32[128,16,8,128]{3,2,1,0:T(8,128)} %bitcast.3.w_ref, f32[16,8,128]{2,1,0:T(8,128)S(1)} %copy-done.5, f32[128,128]{1,0:T(8,128)S(1)} %broadcast_in_dim.2.ritz_ref), custom_call_target="tpu_custom_call" | custom-call | flops 4294967296 | bytes 33554432 | tf_op jit(solution)/shard_map/gram_pair/pallas_call | solution.py:201
  413.7 158.9 %all-to-all-done.2 = f32[8,16,16,8,128]{4,3,2,1,0:T(8,128)} async-done(((f32[8,16,16,8,128]{4,3,2,1,0:T(8,128)}), f32[8,16,16,8,128]{4,3,2,1,0:T(8,128)}, u32[]{:S(2)}, u32[]{:S(2)}) %all-to-all-start.2) | async-done | bytes 8388640 | tf_op jit(solution)/shard_map/all_to_all | solution.py:363
  576.0 12.6 %gram_row.1 = f32[128,384]{1,0:T(8,128)S(1)} custom-call(bf16[256,16384]{1,0:T(8,128)(2,1)S(1)} %copy-done.1, bf16[256,16384]{1,0:T(8,128)(2,1)} %get-tuple-element.16.low_ref, f32[128,16,8,128]{3,2,1,0:T(8,128)} %bitcast.8.d_ref), custom_call_target="tpu_custom_call" | custom-call | flops 4831838208 | bytes 25165824 | tf_op jit(solution)/shard_map/gram_row/pallas_call | solution.py:222
  592.0 5.5 collective-permute-done.8
  598.9 4.8 collective-permute-done.9
  608.0 5.1 collective-permute-done.10
  614.0 11.4 %collective-permute-done.16 = f32[256,256]{1,0:T(8,128)S(1)} collective-permute-done((f32[256,256]{1,0:T(8,128)S(1)}, f32[256,256]{1,0:T(8,128)S(1)}, u32[]{:S(2)}, u32[]{:S(2)}) %collective-permute-start.16) | collective-permute-done | bytes 262176 | tf_op jit(solution)/shard_map/ppermute | solution.py:39
  626.2 14.7 %factor_pair.1.pair_ref = f32[256,256]{1,0:T(8,128)} custom-call(f32[256,256]{1,0:T(8,128)} %add.68.g_ref), custom_call_target="tpu_custom_call" | custom-call | flops 100000000 | bytes 262144 | tf_op jit(solution)/shard_map/factor_pair/pallas_call | solution.py:319
  641.5 9.7 %coefficients.1.c_ref = f32[128,384]{1,0:T(8,128)} custom-call(f32[128,384]{1,0:T(8,128)} %add.63.row_ref, f32[256,256]{1,0:T(8,128)} %factor_pair.1.pair_ref, f32[128,384]{1,0:T(8,128)} %bitcast.18), custom_call_target="tpu_custom_call" | custom-call | flops 100000000 | bytes 196608 | tf_op jit(solution)/shard_map/coefficients/pallas_call | solution.py:338
  655.6 15.0 %apply_basis.1 = f32[128,16,8,128]{3,2,1,0:T(8,128)} custom-call(bf16[256,16384]{1,0:T(8,128)(2,1)S(1)} %copy-done.2, bf16[256,16384]{1,0:T(8,128)(2,1)} %get-tuple-element.16.low_ref, f32[128,16,8,128]{3,2,1,0:T(8,128)} %bitcast.8.d_ref, f32[128,384]{1,0:T(8,128)S(1)} %copy-done.4), custom_call_target="tpu_custom_call" | custom-call | flops 4831838208 | bytes 33554432 | tf_op jit(solution)/shard_map/apply_basis/pallas_call | solution.py:239
  (65 shorter events, 40.8 us)
Async XLA Ops:
  7.8 190.4 %all-to-all-start.1 = ((f32[8,16,16,8,128]{4,3,2,1,0:T(8,128)}), f32[8,16,16,8,128]{4,3,2,1,0:T(8,128)}, u32[]{:S(2)}, u32[]{:S(2)}) async-start(f32[8,16,16,8,128]{4,3,2,1,0:T(8,128)} %copy_bitcast_fusion.1), calls=%async_computation.1 | async-start | bytes 16777216 | tf_op jit(solution)/shard_map/all_to_all | solution.py:363
  19.0 68.6 %collective-permute-start = (f32[16,6,64,128]{3,2,1,0:T(8,128)S(1)}, f32[16,6,64,128]{3,2,1,0:T(8,128)S(1)}, u32[]{:S(2)}, u32[]{:S(2)}) collective-permute-start(f32[16,6,64,128]{3,2,1,0:T(8,128)S(1)} %get-tuple-element.22), channel_id=1, source_target_pairs={{0,8},{8,16},{16,24},{24,0},{1,9},{9,17},{17,25},{25,1},{2,10},{10... | collective-permute-start | bytes 9437192 | tf_op jit(solution)/shard_map/ppermute | solution.py:32
  19.1 69.4 %collective-permute-start.1 = (f32[16,6,64,128]{3,2,1,0:T(8,128)S(1)}, f32[16,6,64,128]{3,2,1,0:T(8,128)S(1)}, u32[]{:S(2)}, u32[]{:S(2)}) collective-permute-start(f32[16,6,64,128]{3,2,1,0:T(8,128)S(1)} %get-tuple-element.21), channel_id=1, source_target_pairs={{8,0},{16,8},{24,16},{0,24},{9,1},{17,9},{25,17},{1,25},{10,2},{18... | collective-permute-start | bytes 9437192 | tf_op jit(solution)/shard_map/ppermute | solution.py:32
  136.6 3.4 copy-start.3
  198.2 5.4 copy-start.5
  198.2 187.4 %all-to-all-start = ((f32[8,16,16,8,128]{4,3,2,1,0:T(8,128)}), f32[8,16,16,8,128]{4,3,2,1,0:T(8,128)}, u32[]{:S(2)}, u32[]{:S(2)}) async-start(f32[8,16,16,8,128]{4,3,2,1,0:T(8,128)} %copy-done.3), calls=%async_computation | async-start | bytes 16777216 | tf_op jit(solution)/shard_map/all_to_all | solution.py:363
  209.1 1.2 collective-permute-start.2
  210.3 3.6 collective-permute-start.3
  214.0 56.4 %collective-permute-start.4 = (f32[2,128]{1,0:T(2,128)S(1)}, f32[2,128]{1,0:T(2,128)S(1)}, u32[]{:S(2)}, u32[]{:S(2)}) collective-permute-start(f32[2,128]{1,0:T(2,128)S(1)} %fusion.3), channel_id=1, source_target_pairs={{0,1},{1,0},{2,3},{3,2},{4,5},{5,4},{6,7},{7,6},{8,9},{9,8},{10,11... | collective-permute-start | bytes 3080 | tf_op jit(solution)/shard_map/ppermute | solution.py:39
  270.4 67.9 %collective-permute-start.5 = (f32[2,128]{1,0:T(2,128)S(1)}, f32[2,128]{1,0:T(2,128)S(1)}, u32[]{:S(2)}, u32[]{:S(2)}) collective-permute-start(f32[2,128]{1,0:T(2,128)S(1)} %add.56), channel_id=1, source_target_pairs={{0,2},{1,3},{2,0},{3,1},{4,6},{5,7},{6,4},{7,5},{8,10},{9,11},{10,... | collective-permute-start | bytes 3080 | tf_op jit(solution)/shard_map/ppermute | solution.py:39
  338.3 47.3 %collective-permute-start.6 = (f32[2,128]{1,0:T(2,128)S(1)}, f32[2,128]{1,0:T(2,128)S(1)}, u32[]{:S(2)}, u32[]{:S(2)}) collective-permute-start(f32[2,128]{1,0:T(2,128)S(1)} %add.57), channel_id=1, source_target_pairs={{0,4},{1,5},{2,6},{3,7},{4,0},{5,1},{6,2},{7,3},{8,12},{9,13},{10,... | collective-permute-start | bytes 3080 | tf_op jit(solution)/shard_map/ppermute | solution.py:39
  385.7 187.0 %all-to-all-start.2 = ((f32[8,16,16,8,128]{4,3,2,1,0:T(8,128)}), f32[8,16,16,8,128]{4,3,2,1,0:T(8,128)}, u32[]{:S(2)}, u32[]{:S(2)}) async-start(f32[8,16,16,8,128]{4,3,2,1,0:T(8,128)} %copy_bitcast_fusion), calls=%async_computation.2 | async-start | bytes 16777216 | tf_op jit(solution)/shard_map/all_to_all | solution.py:363
  407.1 3.4 copy-start
  410.5 1.5 collective-permute-start.12
  412.1 176.7 %collective-permute-start.13 = (f32[256,256]{1,0:T(8,128)S(1)}, f32[256,256]{1,0:T(8,128)S(1)}, u32[]{:S(2)}, u32[]{:S(2)}) collective-permute-start(f32[256,256]{1,0:T(8,128)S(1)} %add.64), channel_id=1, source_target_pairs={{0,16},{8,24},{16,0},{24,8},{1,17},{9,25},{17,1},{25,9},{2,18},{10... | collective-permute-start | bytes 786440 | tf_op jit(solution)/shard_map/ppermute | solution.py:39
  576.0 37.2 %copy-start.6 = (f32[384,128]{1,0:T(8,128)S(1)}, f32[384,128]{1,0:T(8,128)}, u32[]{:S(2)}) copy-start(f32[384,128]{1,0:T(8,128)} %param.7) | copy-start | bytes 589828
  588.7 1.7 collective-permute-start.7
  588.8 10.0 %collective-permute-start.14 = (f32[256,256]{1,0:T(8,128)S(1)}, f32[256,256]{1,0:T(8,128)S(1)}, u32[]{:S(2)}, u32[]{:S(2)}) collective-permute-start(f32[256,256]{1,0:T(8,128)S(1)} %add.65), channel_id=1, source_target_pairs={{0,1},{1,0},{2,3},{3,2},{4,5},{5,4},{6,7},{7,6},{8,9},{9,8},{10,11... | collective-permute-start | bytes 786440 | tf_op jit(solution)/shard_map/ppermute | solution.py:39
  590.4 7.1 %collective-permute-start.8 = (f32[128,384]{1,0:T(8,128)S(1)}, f32[128,384]{1,0:T(8,128)S(1)}, u32[]{:S(2)}, u32[]{:S(2)}) collective-permute-start(f32[128,384]{1,0:T(8,128)S(1)} %add.59), channel_id=1, source_target_pairs={{0,16},{8,24},{16,0},{24,8},{1,17},{9,25},{17,1},{25,9},{2,18},{10... | collective-permute-start | bytes 589832 | tf_op jit(solution)/shard_map/ppermute | solution.py:39
  597.5 6.3 collective-permute-start.9
  598.8 8.5 %collective-permute-start.15 = (f32[256,256]{1,0:T(8,128)S(1)}, f32[256,256]{1,0:T(8,128)S(1)}, u32[]{:S(2)}, u32[]{:S(2)}) collective-permute-start(f32[256,256]{1,0:T(8,128)S(1)} %add.66), channel_id=1, source_target_pairs={{0,2},{1,3},{2,0},{3,1},{4,6},{5,7},{6,4},{7,5},{8,10},{9,11},{10,... | collective-permute-start | bytes 786440 | tf_op jit(solution)/shard_map/ppermute | solution.py:39
  603.8 9.4 %collective-permute-start.10 = (f32[128,384]{1,0:T(8,128)S(1)}, f32[128,384]{1,0:T(8,128)S(1)}, u32[]{:S(2)}, u32[]{:S(2)}) collective-permute-start(f32[128,384]{1,0:T(8,128)S(1)} %add.61), channel_id=1, source_target_pairs={{0,2},{1,3},{2,0},{3,1},{4,6},{5,7},{6,4},{7,5},{8,10},{9,11},{10,... | collective-permute-start | bytes 589832 | tf_op jit(solution)/shard_map/ppermute | solution.py:39
  607.4 18.1 %collective-permute-start.16 = (f32[256,256]{1,0:T(8,128)S(1)}, f32[256,256]{1,0:T(8,128)S(1)}, u32[]{:S(2)}, u32[]{:S(2)}) collective-permute-start(f32[256,256]{1,0:T(8,128)S(1)} %add.67), channel_id=1, source_target_pairs={{0,4},{1,5},{2,6},{3,7},{4,0},{5,1},{6,2},{7,3},{8,12},{9,13},{10,... | collective-permute-start | bytes 786440 | tf_op jit(solution)/shard_map/ppermute | solution.py:39
  613.1 27.7 %collective-permute-start.11 = (f32[128,384]{1,0:T(8,128)S(1)}, f32[128,384]{1,0:T(8,128)S(1)}, u32[]{:S(2)}, u32[]{:S(2)}) collective-permute-start(f32[128,384]{1,0:T(8,128)S(1)} %add.62), channel_id=1, source_target_pairs={{0,4},{1,5},{2,6},{3,7},{4,0},{5,1},{6,2},{7,3},{8,12},{9,13},{10,... | collective-permute-start | bytes 589832 | tf_op jit(solution)/shard_map/ppermute | solution.py:39
  (3 other events, 7.7 us)

commit v2 on v1

--- a/solution.py
+++ b/solution.py
@@ -43,6 +43,24 @@
     return value
 
 
+def halved_sum(value):
+    half = value.shape[0] // 2
+    bands, odd = lax.axis_size("band"), lax.axis_index("band") % 2 == 1
+    swap = [(i, i ^ 1) for i in range(bands)]
+    top, bottom = value[:half], value[half:]
+    mine = jnp.where(odd, bottom, top)
+    mine = mine + lax.ppermute(jnp.where(odd, top, bottom), "band", swap)
+    for axis, step in (("band", 2), ("grid", 1)):
+        devices = lax.axis_size(axis)
+        while step < devices:
+            mine = mine + lax.ppermute(
+                mine, axis, [(i, i ^ step) for i in range(devices)]
+            )
+            step *= 2
+    other = lax.ppermute(mine, "band", swap)
+    return jnp.concatenate([jnp.where(odd, other, mine), jnp.where(odd, mine, other)])
+
+
 def kinetic_kernel(weights, w_ref, lo_ref, hi_ref, t_ref, s_ref, pad):
     _, planes, rows, depth = w_ref.shape
     parts, _, _, mine, _ = t_ref.shape
@@ -121,9 +139,9 @@
     return jnp.concatenate(highs, axis=1), jnp.concatenate(lows, axis=1)
 
 
-def gram_pair_kernel(t_ref, w_ref, v_ref, ritz_ref, g_ref, high_ref, low_ref, acc, cross):
+def gram_pair_kernel(t_ref, w_ref, v_ref, ritz_ref, g_ref, parts_ref, acc, cross):
     step, last = pl.program_id(0), pl.num_programs(0) - 1
-    _, planes, mine, depth = w_ref.shape
+    bands, planes, mine, depth = w_ref.shape
 
     @pl.when(step == 0)
     def _():
@@ -135,47 +153,44 @@
         x, y = i // mine, i % mine
         r = row_of(t_ref, i) + (v_ref[x, y : y + 1, :] - ritz_ref[...]) * w
         high, low = split(jnp.concatenate([r, w], axis=0))
-        high_ref[:, i * depth : (i + 1) * depth] = high
-        low_ref[:, i * depth : (i + 1) * depth] = low
-    high = high_ref[...]
+        parts_ref[: 2 * bands, i * depth : (i + 1) * depth] = high
+        parts_ref[2 * bands :, i * depth : (i + 1) * depth] = low
+    high = parts_ref[: 2 * bands]
     acc[...] += dot_t(high, high)
-    cross[...] += dot_t(high, low_ref[...])
+    cross[...] += dot_t(high, parts_ref[2 * bands :])
 
     @pl.when(step == last)
     def _():
         g_ref[...] = acc[...] + (cross[...] + cross[...].T)
 
 
-def gram_row_kernel(high_ref, low_ref, d_ref, g_ref, acc):
-    step, last = pl.program_id(0), pl.num_programs(0) - 1
-    bands = d_ref.shape[0]
-
-    @pl.when(step == 0)
+def gram_row_kernel(parts_ref, d_ref, so_far_ref, g_ref, both_ref):
+    points = parts_ref.shape[0]
+
+    @pl.when(pl.program_id(0) == 0)
     def _():
-        acc[...] = jnp.zeros_like(acc)
-
-    high, low = split_rows(d_ref)
-    both = jnp.concatenate([high, low], axis=0)
-    wide = dot_t(jnp.concatenate([high_ref[...], high], axis=0), both)
-    acc[...] += wide[:, :bands] + wide[:, bands:]
-    rest = dot_t(jnp.concatenate([low_ref[...], low], axis=0), high)
-    acc[...] += rest
-
-    @pl.when(step == last)
-    def _():
-        g_ref[...] = acc[...].T
-
-
-def apply_kernel(high_ref, low_ref, d_ref, c_ref, o_ref):
+        g_ref[...] = so_far_ref[...]
+
+    both = jnp.concatenate(split_rows(d_ref), axis=0)
+    both_ref[...] = both
+    g_ref[:, :points] += dot_t(both, parts_ref[...])
+    g_ref[:, points:] += dot_t(both, both)
+
+
+def apply_points(parts, both, c_ref, o_ref):
     bands, planes, mine, depth = o_ref.shape
-    d_high, d_low = split_rows(d_ref)
-    c_high, c_low = split(c_ref[...])
-    wide = dot(
-        jnp.concatenate([c_high, c_low], axis=0),
-        jnp.concatenate([high_ref[...], d_high], axis=0),
+    high, low = split(c_ref[...])
+    pair, last = slice(0, 2 * bands), slice(2 * bands, 3 * bands)
+    stacked = jnp.concatenate([high[:, pair], low[:, pair]], axis=0)
+    ending = jnp.concatenate(
+        [
+            jnp.concatenate([high[:, last], high[:, last]], axis=1),
+            jnp.concatenate([low[:, last], jnp.zeros_like(low[:, last])], axis=1),
+        ],
+        axis=0,
     )
-    out = wide[:bands] + wide[bands:]
-    out += dot(c_high, jnp.concatenate([low_ref[...], d_low], axis=0))
+    wide = dot(stacked, parts[: 2 * bands]) + dot(ending, both)
+    out = wide[:bands] + wide[bands:] + dot(high[:, pair], parts[2 * bands :])
     flat = o_ref.reshape(bands * planes * mine, depth)
     for i in range(planes * mine):
         flat[pl.ds(i, bands, stride=planes * mine), :] = out[:, i * depth : (i + 1) * depth]
@@ -190,13 +205,14 @@
 
 
 STEP = 2
+EARLY = 12
 
 
 def gram_pair(t, w, v, ritz):
     bands, planes, mine, depth = w.shape
     tile = tile_spec(bands, STEP, mine, depth)
-    points = pl.BlockSpec((2 * bands, STEP * mine * depth), lambda x: (0, x))
-    parts = jax.ShapeDtypeStruct((2 * bands, planes * mine * depth), BF16)
+    points = pl.BlockSpec((4 * bands, STEP * mine * depth), lambda x: (0, x))
+    parts = jax.ShapeDtypeStruct((4 * bands, planes * mine * depth), BF16)
     square = (2 * bands, 2 * bands)
     return pl.pallas_call(
         gram_pair_kernel,
@@ -207,45 +223,44 @@
             pl.BlockSpec((STEP, mine, depth), lambda x: (x, 0, 0)),
             pl.BlockSpec((bands, depth), lambda x: (0, 0)),
         ],
-        out_specs=[pl.BlockSpec(square, lambda x: (0, 0)), points, points],
-        out_shape=[jax.ShapeDtypeStruct(square, F32), parts, parts],
+        out_specs=[pl.BlockSpec(square, lambda x: (0, 0)), points],
+        out_shape=[jax.ShapeDtypeStruct(square, F32), parts],
         scratch_shapes=[pltpu.VMEM(square, F32), pltpu.VMEM(square, F32)],
-        compiler_params=pltpu.CompilerParams(vmem_limit_bytes=40 << 20),
+        compiler_params=pltpu.CompilerParams(vmem_limit_bytes=60 << 20),
         cost_estimate=cost(16 * bands * w.size, 16 * w.size),
         name="gram_pair",
     )(t, w, v, ritz)
 
 
-def gram_row(high, low, d):
+def gram_row(parts, d, so_far, skip):
     bands, planes, mine, depth = d.shape
-    points = pl.BlockSpec((2 * bands, STEP * mine * depth), lambda x: (0, x))
+    count = STEP * mine * depth
+    whole = pl.BlockSpec(so_far.shape, lambda x: (0, 0))
     return pl.pallas_call(
         gram_row_kernel,
         grid=(planes // STEP,),
-        in_specs=[points, points, tile_spec(bands, STEP, mine, depth)],
-        out_specs=pl.BlockSpec((bands, 3 * bands), lambda x: (0, 0)),
-        out_shape=jax.ShapeDtypeStruct((bands, 3 * bands), F32),
-        scratch_shapes=[pltpu.VMEM((3 * bands, bands), F32)],
-        compiler_params=pltpu.CompilerParams(vmem_limit_bytes=40 << 20),
+        in_specs=[
+            pl.BlockSpec((4 * bands, count), lambda x: (0, x + skip // STEP)),
+            tile_spec(bands, STEP, mine, depth),
+            whole,
+        ],
+        out_specs=[whole, pl.BlockSpec((2 * bands, count), lambda x: (0, x))],
+        out_shape=[
+            jax.ShapeDtypeStruct(so_far.shape, F32),
+            jax.ShapeDtypeStruct((2 * bands, planes * mine * depth), BF16),
+        ],
+        compiler_params=pltpu.CompilerParams(vmem_limit_bytes=(60 if skip == 0 else 40) << 20),
         cost_estimate=cost(18 * bands * d.size, 12 * d.size),
         name="gram_row",
-    )(high, low, d)
-
-
-def apply_basis(high, low, d, coefficients):
-    bands, planes, mine, depth = d.shape
-    points = pl.BlockSpec((2 * bands, STEP * mine * depth), lambda x: (0, x))
-    tile = tile_spec(bands, STEP, mine, depth)
-    return pl.pallas_call(
-        apply_kernel,
-        grid=(planes // STEP,),
-        in_specs=[points, points, tile, pl.BlockSpec((bands, 3 * bands), lambda x: (0, 0))],
-        out_specs=tile,
-        out_shape=jax.ShapeDtypeStruct(d.shape, F32),
-        compiler_params=pltpu.CompilerParams(vmem_limit_bytes=40 << 20),
-        cost_estimate=cost(18 * bands * d.size, 16 * d.size),
-        name="apply_basis",
-    )(high, low, d, coefficients)
+    )(parts, d, so_far)
+
+
+def joined(products):
+    bands = products.shape[0] // 2
+    wide = products[:bands] + products[bands:]
+    pair = wide[:, : 2 * bands] + wide[:, 2 * bands : 4 * bands]
+    own = wide[:, 4 * bands : 5 * bands] + wide[:, 5 * bands :]
+    return jnp.concatenate([pair, own], axis=1)
 
 
 def spread_row(value, i):
@@ -304,11 +319,15 @@
     return jnp.concatenate(done, axis=0)
 
 
-def factor_pair_kernel(scale, g_ref, o_ref):
-    half = g_ref.shape[0] // 2
-    first = inverse_factor(g_ref[:half, :half] * scale)
-    lower = dot_t(g_ref[half:, :half] * scale, first, HIGH)
-    second = inverse_factor(g_ref[half:, half:] * scale - dot_t(lower, lower, HIGH))
+def factor_first_kernel(scale, g_ref, o_ref):
+    o_ref[...] = inverse_factor(g_ref[...] * scale)
+
+
+def factor_second_kernel(scale, g_ref, first_ref, o_ref):
+    half = first_ref.shape[0]
+    first = first_ref[...]
+    lower = dot_t(g_ref[:, :half] * scale, first, HIGH)
+    second = inverse_factor(g_ref[:, half:] * scale - dot_t(lower, lower, HIGH))
     o_ref[:half, :half] = first
     o_ref[:half, half:] = jnp.zeros((half, half), F32)
     o_ref[half:, :half] = -dot(second, dot(lower, first, HIGH), HIGH)
@@ -316,31 +335,79 @@
 
 
 def factor_pair(gram, scale):
+    half = gram.shape[0] // 2
+    first = pl.pallas_call(
+        functools.partial(factor_first_kernel, scale),
+        grid=(1,),
+        in_specs=[pl.BlockSpec((half, half), lambda i: (0, 0))],
+        out_specs=pl.BlockSpec((half, half), lambda i: (0, 0)),
+        out_shape=jax.ShapeDtypeStruct((half, half), F32),
+        cost_estimate=cost(10**9, gram.size),
+        name="factor_first",
+    )(gram)
     return pl.pallas_call(
-        functools.partial(factor_pair_kernel, scale),
+        functools.partial(factor_second_kernel, scale),
+        grid=(1,),
+        in_specs=[
+            pl.BlockSpec((half, 2 * half), lambda i: (1, 0)),
+            pl.BlockSpec((half, half), lambda i: (0, 0)),
+        ],
+        out_specs=pl.BlockSpec((2 * half, 2 * half), lambda i: (0, 0)),
         out_shape=jax.ShapeDtypeStruct(gram.shape, F32),
-        cost_estimate=cost(10**8, 4 * gram.size),
-        name="factor_pair",
-    )(gram)
-
-
-def coefficients_kernel(scale, row_ref, pair_ref, turned_ref, o_ref):
-    bands = row_ref.shape[0]
-    pair = pair_ref[...]
-    lower = dot_t(row_ref[:, : 2 * bands] * scale, pair, HIGH)
-    last = inverse_factor(row_ref[:, 2 * bands :] * scale - dot_t(lower, lower, HIGH))
-    tail = dot(turned_ref[:, 2 * bands :], last, HIGH)
-    o_ref[:, 2 * bands :] = tail
-    o_ref[:, : 2 * bands] = dot(turned_ref[:, : 2 * bands] - dot(tail, lower, HIGH), pair, HIGH)
-
-
-def coefficients_of(row, pair, turned, scale):
+        cost_estimate=cost(10**9, 4 * gram.size),
+        name="factor_second",
+    )(gram, first)
+
+
+def finish_kernel(scale, row_ref, pair_ref, turned_ref, parts_hbm, early_hbm, late_hbm, o_ref, *scratch):
+    parts_ref, both_ref, c_ref, sems = scratch
+    step, bands = pl.program_id(0), row_ref.shape[0]
+    count = parts_ref.shape[1] // pl.num_programs(0)
+    cut = early_hbm.shape[1] // count
+
+    @pl.when(step == 0)
+    def _():
+        for i in range(parts_ref.shape[1] // count):
+            to = pl.ds(i * count, count)
+            d_hbm, at = (early_hbm, i) if i < cut else (late_hbm, i - cut)
+            own = d_hbm.at[:, pl.ds(at * count, count)]
+            pltpu.make_async_copy(parts_hbm.at[:, to], parts_ref.at[:, to], sems.at[0, i]).start()
+            pltpu.make_async_copy(own, both_ref.at[:, to], sems.at[1, i]).start()
+        pair = pair_ref[...]
+        lower = dot_t(row_ref[:, : 2 * bands] * scale, pair, HIGH)
+        last = inverse_factor(row_ref[:, 2 * bands :] * scale - dot_t(lower, lower, HIGH))
+        tail = dot(turned_ref[:, 2 * bands :], last, HIGH)
+        c_ref[:, 2 * bands :] = tail
+        rest = turned_ref[:, : 2 * bands] - dot(tail, lower, HIGH)
+        c_ref[:, : 2 * bands] = dot(rest, pair, HIGH)
+
+    here = pl.ds(pl.multiple_of(step * count, count), count)
+    for to_ref, sem in ((parts_ref, sems.at[0, step]), (both_ref, sems.at[1, step])):
+        pltpu.make_async_copy(to_ref.at[:, here], to_ref.at[:, here], sem).wait()
+    apply_points(parts_ref[:, here], both_ref[:, here], c_ref, o_ref)
+
+
+def finish(row, pair, turned, parts, early, late, scale, mine, depth):
+    bands, points = row.shape[0], parts.shape[1]
+    planes = points // (mine * depth)
+    far = pl.BlockSpec(memory_space=pl.ANY)
+    whole = lambda a: pl.BlockSpec(a.shape, lambda x: (0, 0), pipeline_mode=pl.Buffered(1))
     return pl.pallas_call(
-        functools.partial(coefficients_kernel, scale),
-        out_shape=jax.ShapeDtypeStruct(row.shape, F32),
-        cost_estimate=cost(10**8, 4 * row.size),
-        name="coefficients",
-    )(row, pair, turned)
+        functools.partial(finish_kernel, scale),
+        grid=(planes // STEP,),
+        in_specs=[whole(row), whole(pair), whole(turned), far, far, far],
+        out_specs=pl.BlockSpec((bands, STEP, mine, depth), lambda x: (0, x, 0, 0)),
+        out_shape=jax.ShapeDtypeStruct((bands, planes, mine, depth), F32),
+        scratch_shapes=[
+            pltpu.VMEM(parts.shape, BF16),
+            pltpu.VMEM((2 * bands, points), BF16),
+            pltpu.VMEM(row.shape, F32),
+            pltpu.SemaphoreType.DMA((2, planes // STEP)),
+        ],
+        compiler_params=pltpu.CompilerParams(vmem_limit_bytes=60 << 20),
+        cost_estimate=cost(18 * parts.size * bands // 4, 4 * parts.size),
+        name="finish",
+    )(row, pair, turned, parts, early, late)
 
 
 def fast(wave, direction, potential, rotation):
@@ -356,12 +423,12 @@
     ncells = total_x * rows_y * depth
 
     def pack(field):
-        cut = field.reshape(bands_here, planes, parts, mine, depth)
+        cut = field.reshape(bands_here, -1, parts, mine, depth)
         return cut.transpose(2, 0, 1, 3, 4)
 
     def exchange(blocks):
         got = lax.all_to_all(blocks, "grid", 0, 0, tiled=True)
-        return got.reshape(bands, planes, mine, depth)
+        return got.reshape(bands, -1, mine, depth)
 
     before, after = halos(wave, "band", 1)
     w = exchange(pack(wave))
@@ -375,17 +442,22 @@
     numer = own + jnp.sum(square * potential[None], axis=(1, 2, 3))
     sums = butterfly_sum(jnp.stack([numer, jnp.sum(square, axis=(1, 2, 3))]))
     t = exchange(sent)
-    d_sent, sums = lax.optimization_barrier((pack(direction), sums))
+    cut = EARLY * planes // 16
+    early, late, sums, turned = lax.optimization_barrier(
+        (pack(direction[:, :cut]), pack(direction[:, cut:]), sums, rotation.T)
+    )
     ritz = jnp.broadcast_to((sums[0] / sums[1])[:, None], (bands, depth))
-    d = exchange(d_sent)
-
-    pair, high, low = gram_pair(t, w, potential, ritz)
-    pair = butterfly_sum(pair)
-    row = gram_row(high, low, d)
+    early = exchange(early)
+    pair, basis = gram_pair(t, w, potential, ritz)
+    late, pair = lax.optimization_barrier((late, halved_sum(pair)))
+    late = exchange(late)
+
     inverse = factor_pair(pair, 1.0 / ncells)
-    row = butterfly_sum(row)
-    solved = coefficients_of(row, inverse, rotation.T, 1.0 / ncells)
-    return apply_basis(high, low, d, solved)
+    row, early = gram_row(basis, early, jnp.zeros((2 * bands, 6 * bands), F32), 0)
+    late, row, inverse = lax.optimization_barrier((late, row, inverse))
+    row, late = gram_row(basis, late, row, cut)
+    row = halved_sum(joined(row))
+    return finish(row, inverse, turned, basis, early, late, 1.0 / ncells, mine, depth)
 
 
 def axis_term(field, axis):
@@ -431,7 +503,9 @@
 def on_device(wave, direction, potential, rotation):
     _, planes, rows_y, depth = wave.shape
     mine = rows_y // lax.axis_size("grid")
-    tiled = mine == 8 and depth == 128 and planes % STEP == 0
+    sizes = lax.axis_size("band"), lax.axis_size("grid")
+    tiled = mine == 8 and depth == 128 and planes % (8 * STEP) == 0
+    tiled = tiled and all(n & (n - 1) == 0 for n in sizes) and sizes[0] > 1
     return (fast if tiled else general)(wave, direction, potential, rotation)
 
 

time: 672 us -> 640 us (0.952)
  waiting for transfers between devices: 476 us -> 437 us
  starting transfers between devices: 35.3 us -> 44.3 us
    all_to_all x3 -> x4, waiting for transfers between devices: 217 us -> 78 us  [exchange(): got = lax.all_to_all(blocks, 'grid', 0, 0, tiled=True)]
    ppermute x0 -> x12, waiting for transfers between devices: none -> 134 us  [the longest x8 129 us: halved_sum(): lax.ppermute(mine, axis, [(i, i ^ step) for i in range(devices)])]
    ppermute x15 -> x5, waiting for transfers between devices: 191 us -> 157 us  [butterfly_sum(): lax.ppermute(value, axis, [(i, i ^ step) for i in range(devices)])]
    ppermute x0 -> x12, starting transfers between devices: none -> 12.5 us  [the longest x8 12.2 us: halved_sum(): lax.ppermute(mine, axis, [(i, i ^ step) for i in range(devices)])]
    unnamed x15 -> x11, local copies, waits for them, and re-layouts: 15.3 us -> 6.73 us
    ppermute x15 -> x5, starting transfers between devices: 16 us -> 9.09 us  [butterfly_sum(): lax.ppermute(value, axis, [(i, i ^ step) for i in range(devices)])]
    all_to_all x3 -> x4, starting transfers between devices: 17.4 us -> 20.9 us  [exchange(): got = lax.all_to_all(blocks, 'grid', 0, 0, tiled=True)]
    transpose x2 -> x3, local copies, waits for them, and re-layouts: 15.6 us -> 17.3 us  [pack(): return cut.transpose(2, 0, 1, 3, 4)]
  transfers between devices with their start and end apart: 20 -> 23, of which waited for: 15 -> 21; matrix products, arithmetic and copies ran while one was open for 3% -> 4% of each run, Pallas kernels for 14% -> 15%
where the time goes in v2:
time: 640 us; the launch traced here: 639 us
  waiting for transfers between devices  437 us (68%)
  Pallas kernels  118 us (18%)
  starting transfers between devices  44.3 us (7%)
  local copies, waits for them, and re-layouts  29.9 us (5%)
  other arithmetic  9.01 us (1%)
    ppermute x5, waiting for transfers between devices, butterfly_sum(): lax.ppermute(value, axis, [(i, i ^ step) for i in range(devices)])  157 us
    ppermute x8, waiting for transfers between devices, halved_sum(): lax.ppermute(mine, axis, [(i, i ^ step) for i in range(devices)])  129 us
    all_to_all x4, waiting for transfers between devices, exchange(): got = lax.all_to_all(blocks, 'grid', 0, 0, tiled=True)  78 us
    ppermute x2, waiting for transfers between devices, halos(): return (lax.ppermute(last, axis, up), lax.ppermute(first, axis, down))  67.7 us
    pallas_call x1, Pallas kernels, kinetic(): pl.pallas_call(functools.partial(kinetic_kernel, weights), grid=(bands,),...  48.1 us
    all_to_all x4, starting transfers between devices, exchange(): got = lax.all_to_all(blocks, 'grid', 0, 0, tiled=True)  20.9 us
    pallas_call x1, Pallas kernels, finish(): pl.pallas_call(functools.partial(finish_kernel, scale), grid=(planes // S...  20.6 us
    pallas_call x1, Pallas kernels, gram_pair(): pl.pallas_call(gram_pair_kernel, grid=(planes // STEP,), in_specs=[tile,...  17.9 us
  transfers between devices with their start and end apart: 23, of which 21 were waited for; matrix products, arithmetic and copies ran while one was open for 4% of the time, Pallas kernels for 15%

profile of v2, /device:TPU:0, one launch (start us, length us, event | category | flops | bytes accessed | tf_op | source)
XLA Modules:
  0.0 639.1 jit_solution(11175041185581432385)
XLA Ops:
  0.0 7.8 %copy_bitcast_fusion = f32[8,16,16,8,128]{4,3,2,1,0:T(8,128)} fusion(f32[16,16,64,128]{3,2,1,0:T(8,128)} %w_ref.1), kind=kLoop, calls=%fused_computation | loop fusion | bytes 16777216 | tf_op jit(solution)/shard_map/transpose | solution.py:427
  7.8 7.3 %all-to-all-start.1 = ((f32[8,16,16,8,128]{4,3,2,1,0:T(8,128)}), f32[8,16,16,8,128]{4,3,2,1,0:T(8,128)}, u32[]{:S(2)}, u32[]{:S(2)}) async-start(f32[8,16,16,8,128]{4,3,2,1,0:T(8,128)} %copy_bitcast_fusion), calls=%async_computation.1 | async-start | bytes 16777216 | tf_op jit(solution)/shard_map/all_to_all | solution.py:430
  20.8 66.8 %collective-permute-done.lo_ref = f32[16,6,64,128]{3,2,1,0:T(8,128)S(1)} collective-permute-done((f32[16,6,64,128]{3,2,1,0:T(8,128)S(1)}, f32[16,6,64,128]{3,2,1,0:T(8,128)S(1)}, u32[]{:S(2)}, u32[]{:S(2)}) %collective-permute-start) | collective-permute-done | bytes 3145760 | tf_op jit(solution)/shard_map/ppermute | solution.py:32
  88.5 48.1 %kinetic.1 = (f32[8,16,16,8,128]{4,3,2,1,0:T(8,128)S(1)}, f32[16,8,128]{2,1,0:T(8,128)S(1)}) custom-call(f32[16,16,64,128]{3,2,1,0:T(8,128)} %w_ref.1, f32[16,6,64,128]{3,2,1,0:T(8,128)S(1)} %collective-permute-done.lo_ref, f32[16,6,64,128]{3,2,1,0:T(8,128)S(1)} %collective-permute-done.1.hi_ref), custom_call_target="tpu_custom_call" | custom-call | flops 125829120 | bytes 23068672 | tf_op jit(solution)/shard_map/kinetic/pallas_call | solution.py:92
  140.0 58.2 %all-to-all-done.1 = f32[8,16,16,8,128]{4,3,2,1,0:T(8,128)} async-done(((f32[8,16,16,8,128]{4,3,2,1,0:T(8,128)}), f32[8,16,16,8,128]{4,3,2,1,0:T(8,128)}, u32[]{:S(2)}, u32[]{:S(2)}) %all-to-all-start.1) | async-done | bytes 8388640 | tf_op jit(solution)/shard_map/all_to_all | solution.py:430
  198.2 5.1 all-to-all-start
  203.6 5.1 multiply_reduce_fusion
  216.0 54.3 %collective-permute-done.4 = f32[2,128]{1,0:T(2,128)S(1)} collective-permute-done((f32[2,128]{1,0:T(2,128)S(1)}, f32[2,128]{1,0:T(2,128)S(1)}, u32[]{:S(2)}, u32[]{:S(2)}) %collective-permute-start.4) | collective-permute-done | bytes 1056 | tf_op jit(solution)/shard_map/ppermute | solution.py:39
  271.8 6.2 copy_bitcast_fusion.1
  278.1 60.2 %collective-permute-done.5 = f32[2,128]{1,0:T(2,128)S(1)} collective-permute-done((f32[2,128]{1,0:T(2,128)S(1)}, f32[2,128]{1,0:T(2,128)S(1)}, u32[]{:S(2)}, u32[]{:S(2)}) %collective-permute-start.5) | collective-permute-done | bytes 1056 | tf_op jit(solution)/shard_map/ppermute | solution.py:39
  346.2 39.4 %collective-permute-done.6 = f32[2,128]{1,0:T(2,128)S(1)} collective-permute-done((f32[2,128]{1,0:T(2,128)S(1)}, f32[2,128]{1,0:T(2,128)S(1)}, u32[]{:S(2)}, u32[]{:S(2)}) %collective-permute-start.6) | collective-permute-done | bytes 1056 | tf_op jit(solution)/shard_map/ppermute | solution.py:39
  385.6 4.8 all-to-all-start.3
  391.1 17.9 %gram_pair.1 = (f32[256,256]{1,0:T(8,128)}, bf16[512,16384]{1,0:T(8,128)(2,1)}) custom-call(f32[128,16,8,128]{3,2,1,0:T(8,128)} %bitcast.t_ref, f32[128,16,8,128]{3,2,1,0:T(8,128)} %bitcast.3.w_ref, f32[16,8,128]{2,1,0:T(8,128)} %v_ref.1, f32[128,128]{1,0:T(8,128)} %broadcast_in_dim.4.ritz_ref), custom_call_target="tpu_custom_call" | custom-call | flops 4294967296 | bytes 33554432 | tf_op jit(solution)/shard_map/gram_pair/pallas_call | solution.py:217
  420.0 24.3 %collective-permute-done.9 = f32[128,256]{1,0:T(8,128)S(1)} collective-permute-done((f32[128,256]{1,0:T(8,128)S(1)}, f32[128,256]{1,0:T(8,128)S(1)}, u32[]{:S(2)}, u32[]{:S(2)}) %collective-permute-start.9) | collective-permute-done | bytes 131104 | tf_op jit(solution)/shard_map/ppermute | solution.py:56
  444.7 49.5 %collective-permute-done.10 = f32[128,256]{1,0:T(8,128)S(1)} collective-permute-done((f32[128,256]{1,0:T(8,128)S(1)}, f32[128,256]{1,0:T(8,128)S(1)}, u32[]{:S(2)}, u32[]{:S(2)}) %collective-permute-start.10) | collective-permute-done | bytes 131104 | tf_op jit(solution)/shard_map/ppermute | solution.py:56
  494.2 4.1 collective-permute-start.11
  498.4 34.8 %collective-permute-done.11 = f32[128,256]{1,0:T(8,128)S(1)} collective-permute-done((f32[128,256]{1,0:T(8,128)S(1)}, f32[128,256]{1,0:T(8,128)S(1)}, u32[]{:S(2)}, u32[]{:S(2)}) %collective-permute-start.11) | collective-permute-done | bytes 131104 | tf_op jit(solution)/shard_map/ppermute | solution.py:56
  539.1 7.1 %factor_first.1.first_ref = f32[128,128]{1,0:T(8,128)} custom-call(f32[256,256]{1,0:T(8,128)} %pad_maximum_fusion.g_ref), custom_call_target="tpu_custom_call" | custom-call | flops 1000000000 | bytes 65536 | tf_op jit(solution)/shard_map/factor_first/pallas_call | solution.py:339
  546.2 8.5 %factor_second.1.pair_ref = f32[256,256]{1,0:T(8,128)} custom-call(f32[256,256]{1,0:T(8,128)} %pad_maximum_fusion.g_ref, f32[128,128]{1,0:T(8,128)} %factor_first.1.first_ref), custom_call_target="tpu_custom_call" | custom-call | flops 1000000000 | bytes 262144 | tf_op jit(solution)/shard_map/factor_second/pallas_call | solution.py:348
  555.6 12.2 %gram_row.2 = (f32[256,768]{1,0:T(8,128)}, bf16[256,12288]{1,0:T(8,128)(2,1)}) custom-call(bf16[512,16384]{1,0:T(8,128)(2,1)} %get-tuple-element.25.parts_ref.parts_hbm, f32[128,12,8,128]{3,2,1,0:T(8,128)} %bitcast.12.d_ref, f32[256,768]{1,0:T(8,128)} %broadcast_in_dim.5.so_far_ref), custom_call_target="tpu_custom_call" | custom-call | flops 3623878656 | bytes 18874368 | tf_op jit(solution)/shard_map/gram_row/pallas_call | solution.py:239
  567.9 19.8 %all-to-all-done.2 = f32[8,16,4,8,128]{4,3,2,1,0:T(8,128)S(1)} async-done(((f32[8,16,4,8,128]{4,3,2,1,0:T(8,128)}), f32[8,16,4,8,128]{4,3,2,1,0:T(8,128)S(1)}, u32[]{:S(2)}, u32[]{:S(2)}) %all-to-all-start.2) | async-done | bytes 2097184 | tf_op jit(solution)/shard_map/all_to_all | solution.py:430
  605.5 4.6 collective-permute-done.16
  611.0 5.2 collective-permute-done.17
  618.3 20.6 %finish.1 = f32[128,16,8,128]{3,2,1,0:T(8,128)} custom-call(f32[128,384]{1,0:T(8,128)} %pad_maximum_fusion.1.row_ref, f32[256,256]{1,0:T(8,128)} %factor_second.1.pair_ref, f32[128,384]{1,0:T(8,128)} %bitcast.25, bf16[512,16384]{1,0:T(8,128)(2,1)} %get-tuple-element.25.parts_ref.parts_hbm, bf16[256,12288]{1,0:T(8,128)(2,1)} %get-tuple-element.37.early_hbm, ...), custom_call_target="tpu_custom_call" | custom-call | flops 4831838208 | bytes 33554432 | tf_op jit(solution)/shard_map/finish/pallas_call | solution.py:395
  (79 shorter events, 66.8 us)
Async XLA Ops:
  7.8 190.4 %all-to-all-start.1 = ((f32[8,16,16,8,128]{4,3,2,1,0:T(8,128)}), f32[8,16,16,8,128]{4,3,2,1,0:T(8,128)}, u32[]{:S(2)}, u32[]{:S(2)}) async-start(f32[8,16,16,8,128]{4,3,2,1,0:T(8,128)} %copy_bitcast_fusion), calls=%async_computation.1 | async-start | bytes 16777216 | tf_op jit(solution)/shard_map/all_to_all | solution.py:430
  19.0 68.6 %collective-permute-start = (f32[16,6,64,128]{3,2,1,0:T(8,128)S(1)}, f32[16,6,64,128]{3,2,1,0:T(8,128)S(1)}, u32[]{:S(2)}, u32[]{:S(2)}) collective-permute-start(f32[16,6,64,128]{3,2,1,0:T(8,128)S(1)} %get-tuple-element.42), channel_id=1, source_target_pairs={{0,8},{8,16},{16,24},{24,0},{1,9},{9,17},{17,25},{25,1},{2,10},{10... | collective-permute-start | bytes 9437192 | tf_op jit(solution)/shard_map/ppermute | solution.py:32
  19.1 69.4 %collective-permute-start.1 = (f32[16,6,64,128]{3,2,1,0:T(8,128)S(1)}, f32[16,6,64,128]{3,2,1,0:T(8,128)S(1)}, u32[]{:S(2)}, u32[]{:S(2)}) collective-permute-start(f32[16,6,64,128]{3,2,1,0:T(8,128)S(1)} %get-tuple-element.41), channel_id=1, source_target_pairs={{8,0},{16,8},{24,16},{0,24},{9,1},{17,9},{25,17},{1,25},{10,2},{18... | collective-permute-start | bytes 9437192 | tf_op jit(solution)/shard_map/ppermute | solution.py:32
  198.2 187.4 %all-to-all-start = ((f32[8,16,16,8,128]{4,3,2,1,0:T(8,128)}), f32[8,16,16,8,128]{4,3,2,1,0:T(8,128)}, u32[]{:S(2)}, u32[]{:S(2)}) async-start(f32[8,16,16,8,128]{4,3,2,1,0:T(8,128)} %copy-done), calls=%async_computation | async-start | bytes 16777216 | tf_op jit(solution)/shard_map/all_to_all | solution.py:430
  209.1 1.2 collective-permute-start.2
  210.3 3.6 collective-permute-start.3
  213.9 56.4 %collective-permute-start.4 = (f32[2,128]{1,0:T(2,128)S(1)}, f32[2,128]{1,0:T(2,128)S(1)}, u32[]{:S(2)}, u32[]{:S(2)}) collective-permute-start(f32[2,128]{1,0:T(2,128)S(1)} %fusion.4), channel_id=1, source_target_pairs={{0,1},{1,0},{2,3},{3,2},{4,5},{5,4},{6,7},{7,6},{8,9},{9,8},{10,11... | collective-permute-start | bytes 3080 | tf_op jit(solution)/shard_map/ppermute | solution.py:39
  270.3 75.1 %copy-start.4 = (f32[384,128]{1,0:T(8,128)S(1)}, f32[384,128]{1,0:T(8,128)}, u32[]{:S(2)}) copy-start(f32[384,128]{1,0:T(8,128)} %param.7) | copy-start | bytes 589828
  270.3 67.9 %collective-permute-start.5 = (f32[2,128]{1,0:T(2,128)S(1)}, f32[2,128]{1,0:T(2,128)S(1)}, u32[]{:S(2)}, u32[]{:S(2)}) collective-permute-start(f32[2,128]{1,0:T(2,128)S(1)} %add.71), channel_id=1, source_target_pairs={{0,2},{1,3},{2,0},{3,1},{4,6},{5,7},{6,4},{7,5},{8,10},{9,11},{10,... | collective-permute-start | bytes 3080 | tf_op jit(solution)/shard_map/ppermute | solution.py:39
  338.3 47.3 %collective-permute-start.6 = (f32[2,128]{1,0:T(2,128)S(1)}, f32[2,128]{1,0:T(2,128)S(1)}, u32[]{:S(2)}, u32[]{:S(2)}) collective-permute-start(f32[2,128]{1,0:T(2,128)S(1)} %add.72), channel_id=1, source_target_pairs={{0,4},{1,5},{2,6},{3,7},{4,0},{5,1},{6,2},{7,3},{8,12},{9,13},{10,... | collective-permute-start | bytes 3080 | tf_op jit(solution)/shard_map/ppermute | solution.py:39
  385.6 149.7 %all-to-all-start.3 = ((f32[8,16,12,8,128]{4,3,2,1,0:T(8,128)}), f32[8,16,12,8,128]{4,3,2,1,0:T(8,128)}, u32[]{:S(2)}, u32[]{:S(2)}) async-start(f32[8,16,12,8,128]{4,3,2,1,0:T(8,128)} %copy_bitcast_fusion.1), calls=%async_computation.3 | async-start | bytes 12582912 | tf_op jit(solution)/shard_map/all_to_all | solution.py:430
  410.0 1.4 collective-permute-start.7
  412.4 5.6 collective-permute-start.8
  418.0 26.3 %collective-permute-start.9 = (f32[128,256]{1,0:T(8,128)S(1)}, f32[128,256]{1,0:T(8,128)S(1)}, u32[]{:S(2)}, u32[]{:S(2)}) collective-permute-start(f32[128,256]{1,0:T(8,128)S(1)} %add.75), channel_id=1, source_target_pairs={{0,1},{1,0},{2,3},{3,2},{4,5},{5,4},{6,7},{7,6},{8,9},{9,8},{10,11... | collective-permute-start | bytes 393224 | tf_op jit(solution)/shard_map/ppermute | solution.py:56
  444.3 49.9 %collective-permute-start.10 = (f32[128,256]{1,0:T(8,128)S(1)}, f32[128,256]{1,0:T(8,128)S(1)}, u32[]{:S(2)}, u32[]{:S(2)}) collective-permute-start(f32[128,256]{1,0:T(8,128)S(1)} %add.76), channel_id=1, source_target_pairs={{0,2},{1,3},{2,0},{3,1},{4,6},{5,7},{6,4},{7,5},{8,10},{9,11},{10,... | collective-permute-start | bytes 393224 | tf_op jit(solution)/shard_map/ppermute | solution.py:56
  494.2 38.9 %collective-permute-start.11 = (f32[128,256]{1,0:T(8,128)S(1)}, f32[128,256]{1,0:T(8,128)S(1)}, u32[]{:S(2)}, u32[]{:S(2)}) collective-permute-start(f32[128,256]{1,0:T(8,128)S(1)} %add.77), channel_id=1, source_target_pairs={{0,4},{1,5},{2,6},{3,7},{4,0},{5,1},{6,2},{7,3},{8,12},{9,13},{10,... | collective-permute-start | bytes 393224 | tf_op jit(solution)/shard_map/ppermute | solution.py:56
  533.1 1.4 collective-permute-start.12
  535.3 52.4 %all-to-all-start.2 = ((f32[8,16,4,8,128]{4,3,2,1,0:T(8,128)}), f32[8,16,4,8,128]{4,3,2,1,0:T(8,128)S(1)}, u32[]{:S(2)}, u32[]{:S(2)}) async-start(f32[8,16,4,8,128]{4,3,2,1,0:T(8,128)} %copy_bitcast_fusion.2), calls=%async_computation.2 | async-start | bytes 4194304 | tf_op jit(solution)/shard_map/all_to_all | solution.py:430
  594.4 1.4 collective-permute-start.13
  595.8 4.9 collective-permute-start.14
  600.8 4.7 collective-permute-start.15
  605.5 4.7 collective-permute-start.16
  610.2 6.1 collective-permute-start.17
  616.3 1.4 collective-permute-start.18
  (4 other events, 11.3 us)

commit v3 on v2

--- a/solution.py
+++ b/solution.py
@@ -43,21 +43,35 @@
     return value
 
 
-def halved_sum(value):
-    half = value.shape[0] // 2
-    bands, odd = lax.axis_size("band"), lax.axis_index("band") % 2 == 1
-    swap = [(i, i ^ 1) for i in range(bands)]
+def core_pairs():
+    return [(i, i ^ 1) for i in range(lax.axis_size("band"))]
+
+
+def half_of_sum(value):
+    half, odd = value.shape[0] // 2, lax.axis_index("band") % 2 == 1
     top, bottom = value[:half], value[half:]
     mine = jnp.where(odd, bottom, top)
-    mine = mine + lax.ppermute(jnp.where(odd, top, bottom), "band", swap)
-    for axis, step in (("band", 2), ("grid", 1)):
+    mine = mine + lax.ppermute(jnp.where(odd, top, bottom), "band", core_pairs())
+    bands, grids = lax.axis_size("band"), lax.axis_size("grid")
+    flips = [b * grids + g for b in (0, 2) for g in (0, 1)][1:]
+    got = [
+        lax.ppermute(mine, ("band", "grid"), [(i, i ^ f) for i in range(bands * grids)])
+        for f in flips
+    ]
+    mine = (mine + got[0]) + (got[1] + got[2])
+    for axis, step in (("band", 4), ("grid", 2)):
         devices = lax.axis_size(axis)
         while step < devices:
             mine = mine + lax.ppermute(
                 mine, axis, [(i, i ^ step) for i in range(devices)]
             )
             step *= 2
-    other = lax.ppermute(mine, "band", swap)
+    return mine
+
+
+def both_halves(mine):
+    odd = lax.axis_index("band") % 2 == 1
+    other = lax.ppermute(mine, "band", core_pairs())
     return jnp.concatenate([jnp.where(odd, other, mine), jnp.where(odd, mine, other)])
 
 
@@ -164,17 +178,32 @@
         g_ref[...] = acc[...] + (cross[...] + cross[...].T)
 
 
-def gram_row_kernel(parts_ref, d_ref, so_far_ref, g_ref, both_ref):
-    points = parts_ref.shape[0]
-
-    @pl.when(pl.program_id(0) == 0)
+def gram_row_kernel(parts_ref, d_ref, g_ref, both_hbm, held, sems):
+    step, last = pl.program_id(0), pl.num_programs(0) - 1
+    points, count = parts_ref.shape
+
+    @pl.when(step == 0)
     def _():
-        g_ref[...] = so_far_ref[...]
+        g_ref[...] = jnp.zeros_like(g_ref)
+
+    def copy_of(at):
+        to = both_hbm.at[:, pl.ds(pl.multiple_of(at * count, count), count)]
+        return pltpu.make_async_copy(held.at[at % 2], to, sems.at[at % 2])
+
+    @pl.when(step >= 2)
+    def _():
+        copy_of(step - 2).wait()
 
     both = jnp.concatenate(split_rows(d_ref), axis=0)
-    both_ref[...] = both
+    held[step % 2] = both
+    copy_of(step).start()
     g_ref[:, :points] += dot_t(both, parts_ref[...])
     g_ref[:, points:] += dot_t(both, both)
+
+    @pl.when(step == last)
+    def _():
+        copy_of(step - 1).wait()
+        copy_of(step).wait()
 
 
 def apply_points(parts, both, c_ref, o_ref):
@@ -232,35 +261,37 @@
     )(t, w, v, ritz)
 
 
-def gram_row(parts, d, so_far, skip):
+def gram_row(parts, d, skip):
     bands, planes, mine, depth = d.shape
     count = STEP * mine * depth
-    whole = pl.BlockSpec(so_far.shape, lambda x: (0, 0))
-    return pl.pallas_call(
+    shape = (2 * bands, 6 * bands)
+    products, both = pl.pallas_call(
         gram_row_kernel,
         grid=(planes // STEP,),
         in_specs=[
             pl.BlockSpec((4 * bands, count), lambda x: (0, x + skip // STEP)),
             tile_spec(bands, STEP, mine, depth),
-            whole,
-        ],
-        out_specs=[whole, pl.BlockSpec((2 * bands, count), lambda x: (0, x))],
+        ],
+        out_specs=[
+            pl.BlockSpec(shape, lambda x: (0, 0)),
+            pl.BlockSpec(memory_space=pltpu.HBM),
+        ],
         out_shape=[
-            jax.ShapeDtypeStruct(so_far.shape, F32),
+            jax.ShapeDtypeStruct(shape, F32),
             jax.ShapeDtypeStruct((2 * bands, planes * mine * depth), BF16),
+        ],
+        scratch_shapes=[
+            pltpu.VMEM((2, 2 * bands, count), BF16),
+            pltpu.SemaphoreType.DMA((2,)),
         ],
         compiler_params=pltpu.CompilerParams(vmem_limit_bytes=(60 if skip == 0 else 40) << 20),
         cost_estimate=cost(18 * bands * d.size, 12 * d.size),
         name="gram_row",
-    )(parts, d, so_far)
-
-
-def joined(products):
-    bands = products.shape[0] // 2
+    )(parts, d)
     wide = products[:bands] + products[bands:]
     pair = wide[:, : 2 * bands] + wide[:, 2 * bands : 4 * bands]
     own = wide[:, 4 * bands : 5 * bands] + wide[:, 5 * bands :]
-    return jnp.concatenate([pair, own], axis=1)
+    return jnp.concatenate([pair, own], axis=1), both
 
 
 def spread_row(value, i):
@@ -449,14 +480,15 @@
     ritz = jnp.broadcast_to((sums[0] / sums[1])[:, None], (bands, depth))
     early = exchange(early)
     pair, basis = gram_pair(t, w, potential, ritz)
-    late, pair = lax.optimization_barrier((late, halved_sum(pair)))
+    late, half = lax.optimization_barrier((late, half_of_sum(pair)))
     late = exchange(late)
+    pair = both_halves(half)
 
     inverse = factor_pair(pair, 1.0 / ncells)
-    row, early = gram_row(basis, early, jnp.zeros((2 * bands, 6 * bands), F32), 0)
+    row, early = gram_row(basis, early, 0)
     late, row, inverse = lax.optimization_barrier((late, row, inverse))
-    row, late = gram_row(basis, late, row, cut)
-    row = halved_sum(joined(row))
+    late_row, late = gram_row(basis, late, cut)
+    row = both_halves(half_of_sum(row + late_row))
     return finish(row, inverse, turned, basis, early, late, 1.0 / ncells, mine, depth)
 
 
@@ -505,7 +537,7 @@
     mine = rows_y // lax.axis_size("grid")
     sizes = lax.axis_size("band"), lax.axis_size("grid")
     tiled = mine == 8 and depth == 128 and planes % (8 * STEP) == 0
-    tiled = tiled and all(n & (n - 1) == 0 for n in sizes) and sizes[0] > 1
+    tiled = tiled and all(n & (n - 1) == 0 for n in sizes) and sizes[0] >= 4
     return (fast if tiled else general)(wave, direction, potential, rotation)
 
 

time: 640 us -> 636 us (level)
    ppermute x12 -> x14, waiting for transfers between devices: 134 us -> 132 us  [the longest x4 91.3 us: half_of_sum(): lax.ppermute(mine, axis, [(i, i ^ step) for i in range(devices)])]
    ppermute x12 -> x14, starting transfers between devices: 12.5 us -> 12.8 us  [the longest x6 7.11 us: half_of_sum(): lax.ppermute(mine, ('band', 'grid'), [(i, i ^ f) for i in range(bands * g...]
  transfers between devices with their start and end apart: 23 -> 25, of which waited for: 21 -> 22; matrix products, arithmetic and copies ran while one was open for 4% -> 4% of each run, Pallas kernels for 15% -> 15%
where the time goes in v3:
time: 636 us; the launch traced here: 635 us
  waiting for transfers between devices  433 us (68%)
  Pallas kernels  119 us (19%)
  starting transfers between devices  43.6 us (7%)
  local copies, waits for them, and re-layouts  27.9 us (4%)
  other arithmetic  10.3 us (2%)
    ppermute x5, waiting for transfers between devices, butterfly_sum(): lax.ppermute(value, axis, [(i, i ^ step) for i in range(devices)])  157 us
    ppermute x4, waiting for transfers between devices, half_of_sum(): lax.ppermute(mine, axis, [(i, i ^ step) for i in range(devices)])  91.3 us
    all_to_all x4, waiting for transfers between devices, exchange(): got = lax.all_to_all(blocks, 'grid', 0, 0, tiled=True)  74.1 us
    ppermute x2, waiting for transfers between devices, halos(): return (lax.ppermute(last, axis, up), lax.ppermute(first, axis, down))  69.8 us
    pallas_call x1, Pallas kernels, kinetic(): pl.pallas_call(functools.partial(kinetic_kernel, weights), grid=(bands,),...  48.1 us
    ppermute x6, waiting for transfers between devices, half_of_sum(): lax.ppermute(mine, ('band', 'grid'), [(i, i ^ f) for i in range(bands * g...  35.9 us
    all_to_all x4, starting transfers between devices, exchange(): got = lax.all_to_all(blocks, 'grid', 0, 0, tiled=True)  21 us
    pallas_call x1, Pallas kernels, finish(): pl.pallas_call(functools.partial(finish_kernel, scale), grid=(planes // S...  20.6 us
  transfers between devices with their start and end apart: 25, of which 22 were waited for; matrix products, arithmetic and copies ran while one was open for 4% of the time, Pallas kernels for 15%

profile of v3, /device:TPU:0, one launch (start us, length us, event | category | flops | bytes accessed | tf_op | source)
XLA Modules:
  0.0 635.1 jit_solution(12776978417933823654)
XLA Ops:
  0.0 7.8 %copy_bitcast_fusion = f32[8,16,16,8,128]{4,3,2,1,0:T(8,128)} fusion(f32[16,16,64,128]{3,2,1,0:T(8,128)} %w_ref.1), kind=kLoop, calls=%fused_computation | loop fusion | bytes 16777216 | tf_op jit(solution)/shard_map/transpose | solution.py:458
  7.8 7.3 %all-to-all-start = ((f32[8,16,16,8,128]{4,3,2,1,0:T(8,128)}), f32[8,16,16,8,128]{4,3,2,1,0:T(8,128)}, u32[]{:S(2)}, u32[]{:S(2)}) async-start(f32[8,16,16,8,128]{4,3,2,1,0:T(8,128)} %copy_bitcast_fusion), calls=%async_computation | async-start | bytes 16777216 | tf_op jit(solution)/shard_map/all_to_all | solution.py:461
  19.8 68.2 %collective-permute-done.1.hi_ref = f32[16,6,64,128]{3,2,1,0:T(8,128)S(1)} collective-permute-done((f32[16,6,64,128]{3,2,1,0:T(8,128)S(1)}, f32[16,6,64,128]{3,2,1,0:T(8,128)S(1)}, u32[]{:S(2)}, u32[]{:S(2)}) %collective-permute-start.1) | collective-permute-done | bytes 3145760 | tf_op jit(solution)/shard_map/ppermute | solution.py:32
  89.6 48.1 %kinetic.1 = (f32[8,16,16,8,128]{4,3,2,1,0:T(8,128)S(1)}, f32[16,8,128]{2,1,0:T(8,128)S(1)}) custom-call(f32[16,16,64,128]{3,2,1,0:T(8,128)} %w_ref.1, f32[16,6,64,128]{3,2,1,0:T(8,128)S(1)} %collective-permute-done.lo_ref, f32[16,6,64,128]{3,2,1,0:T(8,128)S(1)} %collective-permute-done.1.hi_ref), custom_call_target="tpu_custom_call" | custom-call | flops 125829120 | bytes 23068672 | tf_op jit(solution)/shard_map/kinetic/pallas_call | solution.py:106
  141.0 57.2 %all-to-all-done = f32[8,16,16,8,128]{4,3,2,1,0:T(8,128)} async-done(((f32[8,16,16,8,128]{4,3,2,1,0:T(8,128)}), f32[8,16,16,8,128]{4,3,2,1,0:T(8,128)}, u32[]{:S(2)}, u32[]{:S(2)}) %all-to-all-start) | async-done | bytes 8388640 | tf_op jit(solution)/shard_map/all_to_all | solution.py:461
  198.2 5.1 all-to-all-start.1
  203.6 5.1 multiply_reduce_fusion
  216.0 54.3 %collective-permute-done.4 = f32[2,128]{1,0:T(2,128)S(1)} collective-permute-done((f32[2,128]{1,0:T(2,128)S(1)}, f32[2,128]{1,0:T(2,128)S(1)}, u32[]{:S(2)}, u32[]{:S(2)}) %collective-permute-start.4) | collective-permute-done | bytes 1056 | tf_op jit(solution)/shard_map/ppermute | solution.py:39
  271.8 6.2 copy_bitcast_fusion.1
  278.1 60.2 %collective-permute-done.5 = f32[2,128]{1,0:T(2,128)S(1)} collective-permute-done((f32[2,128]{1,0:T(2,128)S(1)}, f32[2,128]{1,0:T(2,128)S(1)}, u32[]{:S(2)}, u32[]{:S(2)}) %collective-permute-start.5) | collective-permute-done | bytes 1056 | tf_op jit(solution)/shard_map/ppermute | solution.py:39
  346.2 39.4 %collective-permute-done.6 = f32[2,128]{1,0:T(2,128)S(1)} collective-permute-done((f32[2,128]{1,0:T(2,128)S(1)}, f32[2,128]{1,0:T(2,128)S(1)}, u32[]{:S(2)}, u32[]{:S(2)}) %collective-permute-start.6) | collective-permute-done | bytes 1056 | tf_op jit(solution)/shard_map/ppermute | solution.py:39
  385.6 4.8 all-to-all-start.3
  391.1 17.9 %gram_pair.1 = (f32[256,256]{1,0:T(8,128)}, bf16[512,16384]{1,0:T(8,128)(2,1)}) custom-call(f32[128,16,8,128]{3,2,1,0:T(8,128)} %bitcast.8.t_ref, f32[128,16,8,128]{3,2,1,0:T(8,128)} %bitcast.9.w_ref, f32[16,8,128]{2,1,0:T(8,128)} %v_ref.1, f32[128,128]{1,0:T(8,128)} %broadcast_in_dim.2.ritz_ref), custom_call_target="tpu_custom_call" | custom-call | flops 4294967296 | bytes 33554432 | tf_op jit(solution)/shard_map/gram_pair/pallas_call | solution.py:246
  416.0 29.8 %collective-permute-done.10 = f32[128,256]{1,0:T(8,128)S(1)} collective-permute-done((f32[128,256]{1,0:T(8,128)S(1)}, f32[128,256]{1,0:T(8,128)S(1)}, u32[]{:S(2)}, u32[]{:S(2)}) %collective-permute-start.10) | collective-permute-done | bytes 131104 | tf_op jit(solution)/shard_map/ppermute | solution.py:58
  447.6 46.6 %collective-permute-done.11 = f32[128,256]{1,0:T(8,128)S(1)} collective-permute-done((f32[128,256]{1,0:T(8,128)S(1)}, f32[128,256]{1,0:T(8,128)S(1)}, u32[]{:S(2)}, u32[]{:S(2)}) %collective-permute-start.11) | collective-permute-done | bytes 131104 | tf_op jit(solution)/shard_map/ppermute | solution.py:65
  498.3 34.8 %collective-permute-done.12 = f32[128,256]{1,0:T(8,128)S(1)} collective-permute-done((f32[128,256]{1,0:T(8,128)S(1)}, f32[128,256]{1,0:T(8,128)S(1)}, u32[]{:S(2)}, u32[]{:S(2)}) %collective-permute-start.12) | collective-permute-done | bytes 131104 | tf_op jit(solution)/shard_map/ppermute | solution.py:65
  539.1 7.1 %factor_first.1.first_ref = f32[128,128]{1,0:T(8,128)} custom-call(f32[256,256]{1,0:T(8,128)} %pad_maximum_fusion.g_ref), custom_call_target="tpu_custom_call" | custom-call | flops 1000000000 | bytes 65536 | tf_op jit(solution)/shard_map/factor_first/pallas_call | solution.py:370
  546.2 8.5 %factor_second.1.pair_ref = f32[256,256]{1,0:T(8,128)} custom-call(f32[256,256]{1,0:T(8,128)} %pad_maximum_fusion.g_ref, f32[128,128]{1,0:T(8,128)} %factor_first.1.first_ref), custom_call_target="tpu_custom_call" | custom-call | flops 1000000000 | bytes 262144 | tf_op jit(solution)/shard_map/factor_second/pallas_call | solution.py:379
  554.7 12.4 %gram_row.2 = (f32[256,768]{1,0:T(8,128)}, bf16[256,12288]{1,0:T(8,128)(2,1)}) custom-call(bf16[512,16384]{1,0:T(8,128)(2,1)} %get-tuple-element.28.parts_ref.parts_hbm, f32[128,12,8,128]{3,2,1,0:T(8,128)} %bitcast.12.d_ref), custom_call_target="tpu_custom_call" | custom-call | flops 3623878656 | bytes 18874368 | tf_op jit(solution)/shard_map/gram_row/pallas_call | solution.py:268
  568.4 16.9 %all-to-all-done.2 = f32[8,16,4,8,128]{4,3,2,1,0:T(8,128)S(1)} async-done(((f32[8,16,4,8,128]{4,3,2,1,0:T(8,128)}), f32[8,16,4,8,128]{4,3,2,1,0:T(8,128)S(1)}, u32[]{:S(2)}, u32[]{:S(2)}) %all-to-all-start.2) | async-done | bytes 2097184 | tf_op jit(solution)/shard_map/all_to_all | solution.py:461
  585.2 4.9 gram_row.3
  601.1 4.6 collective-permute-done.18
  606.9 5.3 collective-permute-done.19
  614.3 20.6 %finish.1 = f32[128,16,8,128]{3,2,1,0:T(8,128)} custom-call(f32[128,384]{1,0:T(8,128)} %pad_maximum_fusion.2.row_ref, f32[256,256]{1,0:T(8,128)} %factor_second.1.pair_ref, f32[128,384]{1,0:T(8,128)} %bitcast.25, bf16[512,16384]{1,0:T(8,128)(2,1)} %get-tuple-element.28.parts_ref.parts_hbm, bf16[256,12288]{1,0:T(8,128)(2,1)} %get-tuple-element.37.early_hbm, ...), custom_call_target="tpu_custom_call" | custom-call | flops 4831838208 | bytes 33554432 | tf_op jit(solution)/shard_map/finish/pallas_call | solution.py:426
  (83 shorter events, 61.6 us)
Async XLA Ops:
  7.8 190.4 %all-to-all-start = ((f32[8,16,16,8,128]{4,3,2,1,0:T(8,128)}), f32[8,16,16,8,128]{4,3,2,1,0:T(8,128)}, u32[]{:S(2)}, u32[]{:S(2)}) async-start(f32[8,16,16,8,128]{4,3,2,1,0:T(8,128)} %copy_bitcast_fusion), calls=%async_computation | async-start | bytes 16777216 | tf_op jit(solution)/shard_map/all_to_all | solution.py:461
  19.0 68.9 %collective-permute-start.1 = (f32[16,6,64,128]{3,2,1,0:T(8,128)S(1)}, f32[16,6,64,128]{3,2,1,0:T(8,128)S(1)}, u32[]{:S(2)}, u32[]{:S(2)}) collective-permute-start(f32[16,6,64,128]{3,2,1,0:T(8,128)S(1)} %get-tuple-element.41), channel_id=1, source_target_pairs={{8,0},{16,8},{24,16},{0,24},{9,1},{17,9},{25,17},{1,25},{10,2},{18... | collective-permute-start | bytes 9437192 | tf_op jit(solution)/shard_map/ppermute | solution.py:32
  19.8 69.8 %collective-permute-start = (f32[16,6,64,128]{3,2,1,0:T(8,128)S(1)}, f32[16,6,64,128]{3,2,1,0:T(8,128)S(1)}, u32[]{:S(2)}, u32[]{:S(2)}) collective-permute-start(f32[16,6,64,128]{3,2,1,0:T(8,128)S(1)} %get-tuple-element.42), channel_id=1, source_target_pairs={{0,8},{8,16},{16,24},{24,0},{1,9},{9,17},{17,25},{25,1},{2,10},{10... | collective-permute-start | bytes 9437192 | tf_op jit(solution)/shard_map/ppermute | solution.py:32
  198.2 187.4 %all-to-all-start.1 = ((f32[8,16,16,8,128]{4,3,2,1,0:T(8,128)}), f32[8,16,16,8,128]{4,3,2,1,0:T(8,128)}, u32[]{:S(2)}, u32[]{:S(2)}) async-start(f32[8,16,16,8,128]{4,3,2,1,0:T(8,128)} %copy-done), calls=%async_computation.1 | async-start | bytes 16777216 | tf_op jit(solution)/shard_map/all_to_all | solution.py:461
  210.3 3.6 collective-permute-start.3
  213.9 56.4 %collective-permute-start.4 = (f32[2,128]{1,0:T(2,128)S(1)}, f32[2,128]{1,0:T(2,128)S(1)}, u32[]{:S(2)}, u32[]{:S(2)}) collective-permute-start(f32[2,128]{1,0:T(2,128)S(1)} %fusion.3), channel_id=1, source_target_pairs={{0,1},{1,0},{2,3},{3,2},{4,5},{5,4},{6,7},{7,6},{8,9},{9,8},{10,11... | collective-permute-start | bytes 3080 | tf_op jit(solution)/shard_map/ppermute | solution.py:39
  270.3 67.9 %collective-permute-start.5 = (f32[2,128]{1,0:T(2,128)S(1)}, f32[2,128]{1,0:T(2,128)S(1)}, u32[]{:S(2)}, u32[]{:S(2)}) collective-permute-start(f32[2,128]{1,0:T(2,128)S(1)} %add.91), channel_id=1, source_target_pairs={{0,2},{1,3},{2,0},{3,1},{4,6},{5,7},{6,4},{7,5},{8,10},{9,11},{10,... | collective-permute-start | bytes 3080 | tf_op jit(solution)/shard_map/ppermute | solution.py:39
  338.3 47.3 %collective-permute-start.6 = (f32[2,128]{1,0:T(2,128)S(1)}, f32[2,128]{1,0:T(2,128)S(1)}, u32[]{:S(2)}, u32[]{:S(2)}) collective-permute-start(f32[2,128]{1,0:T(2,128)S(1)} %add.92), channel_id=1, source_target_pairs={{0,4},{1,5},{2,6},{3,7},{4,0},{5,1},{6,2},{7,3},{8,12},{9,13},{10,... | collective-permute-start | bytes 3080 | tf_op jit(solution)/shard_map/ppermute | solution.py:39
  385.6 147.5 %all-to-all-start.3 = ((f32[8,16,12,8,128]{4,3,2,1,0:T(8,128)}), f32[8,16,12,8,128]{4,3,2,1,0:T(8,128)}, u32[]{:S(2)}, u32[]{:S(2)}) async-start(f32[8,16,12,8,128]{4,3,2,1,0:T(8,128)} %copy_bitcast_fusion.1), calls=%async_computation.3 | async-start | bytes 12582912 | tf_op jit(solution)/shard_map/all_to_all | solution.py:461
  410.0 1.4 collective-permute-start.7
  412.5 33.4 %collective-permute-start.10 = (f32[128,256]{1,0:T(8,128)S(1)}, f32[128,256]{1,0:T(8,128)S(1)}, u32[]{:S(2)}, u32[]{:S(2)}) collective-permute-start(f32[128,256]{1,0:T(8,128)S(1)} %select_add_fusion), channel_id=1, source_target_pairs={{0,17},{1,16},{2,19},{3,18},{4,21},{5,20},{6,23},{7,22},{8,25},{9,... | collective-permute-start | bytes 393224 | tf_op jit(solution)/shard_map/ppermute | solution.py:58
  415.4 30.5 %collective-permute-start.9 = (f32[128,256]{1,0:T(8,128)S(1)}, f32[128,256]{1,0:T(8,128)S(1)}, u32[]{:S(2)}, u32[]{:S(2)}) collective-permute-start(f32[128,256]{1,0:T(8,128)S(1)} %select_add_fusion), channel_id=1, source_target_pairs={{0,16},{1,17},{2,18},{3,19},{4,20},{5,21},{6,22},{7,23},{8,24},{9,... | collective-permute-start | bytes 393224 | tf_op jit(solution)/shard_map/ppermute | solution.py:58
  415.9 31.6 %collective-permute-start.8 = (f32[128,256]{1,0:T(8,128)S(1)}, f32[128,256]{1,0:T(8,128)S(1)}, u32[]{:S(2)}, u32[]{:S(2)}) collective-permute-start(f32[128,256]{1,0:T(8,128)S(1)} %select_add_fusion), channel_id=1, source_target_pairs={{0,1},{1,0},{2,3},{3,2},{4,5},{5,4},{6,7},{7,6},{8,9},{9,8},{10,11... | collective-permute-start | bytes 393224 | tf_op jit(solution)/shard_map/ppermute | solution.py:58
  447.5 46.7 %collective-permute-start.11 = (f32[128,256]{1,0:T(8,128)S(1)}, f32[128,256]{1,0:T(8,128)S(1)}, u32[]{:S(2)}, u32[]{:S(2)}) collective-permute-start(f32[128,256]{1,0:T(8,128)S(1)} %add_add_fusion), channel_id=1, source_target_pairs={{0,2},{1,3},{2,0},{3,1},{4,6},{5,7},{6,4},{7,5},{8,10},{9,11},{10,... | collective-permute-start | bytes 393224 | tf_op jit(solution)/shard_map/ppermute | solution.py:65
  494.2 38.9 %collective-permute-start.12 = (f32[128,256]{1,0:T(8,128)S(1)}, f32[128,256]{1,0:T(8,128)S(1)}, u32[]{:S(2)}, u32[]{:S(2)}) collective-permute-start(f32[128,256]{1,0:T(8,128)S(1)} %add.98), channel_id=1, source_target_pairs={{0,4},{1,5},{2,6},{3,7},{4,0},{5,1},{6,2},{7,3},{8,12},{9,13},{10,... | collective-permute-start | bytes 393224 | tf_op jit(solution)/shard_map/ppermute | solution.py:65
  533.1 52.1 %all-to-all-start.2 = ((f32[8,16,4,8,128]{4,3,2,1,0:T(8,128)}), f32[8,16,4,8,128]{4,3,2,1,0:T(8,128)S(1)}, u32[]{:S(2)}, u32[]{:S(2)}) async-start(f32[8,16,4,8,128]{4,3,2,1,0:T(8,128)} %copy_bitcast_fusion.2), calls=%async_computation.2 | async-start | bytes 4194304 | tf_op jit(solution)/shard_map/all_to_all | solution.py:461
  536.9 1.4 collective-permute-start.13
  591.6 1.4 collective-permute-start.14
  593.0 5.9 collective-permute-start.17
  595.5 5.5 collective-permute-start.16
  596.0 5.0 collective-permute-start.15
  601.0 4.7 collective-permute-start.18
  605.7 6.5 %collective-permute-start.19 = (f32[64,384]{1,0:T(8,128)S(1)}, f32[64,384]{1,0:T(8,128)S(1)}, u32[]{:S(2)}, u32[]{:S(2)}) collective-permute-start(f32[64,384]{1,0:T(8,128)S(1)} %add.111), channel_id=1, source_target_pairs={{0,4},{1,5},{2,6},{3,7},{4,0},{5,1},{6,2},{7,3},{8,12},{9,13},{10,... | collective-permute-start | bytes 294920 | tf_op jit(solution)/shard_map/ppermute | solution.py:65
  612.2 1.4 collective-permute-start.20
  (5 other events, 86.4 us)

commit v4 on v3

--- a/solution.py
+++ b/solution.py
@@ -308,13 +308,12 @@
     shape = (8, size)
     sublane = lax.broadcasted_iota(jnp.int32, shape, 0)
     lane = lax.broadcasted_iota(jnp.int32, shape, 1)
-    left = [matrix[8 * q : 8 * q + 8] for q in range(count)]
-    right = [jnp.where(lane == sublane + 8 * q, 1.0, 0.0).astype(F32) for q in range(count)]
+    blocks = [matrix[8 * q : 8 * q + 8] for q in range(count)]
     done = []
     for p in range(count):
         base = 8 * p
-        rows = [spread_row(left[p], i) for i in range(8)]
-        ones = [spread_row(right[p], i) for i in range(8)]
+        own = (lane >= base) & (lane < base + 8)
+        rows = [spread_row(blocks[p], i) for i in range(8)]
         entry = {
             (i, j): spread_column(rows[i], base + j) for i in range(8) for j in range(i, 8)
         }
@@ -327,26 +326,24 @@
                 for j in range(i, 8):
                     entry[i, j] = entry[i, j] - unit[i, k] * entry[k, j]
         for i in range(8):
+            rows[i] = jnp.where(own, jnp.where(lane == base + i, 1.0, 0.0), rows[i])
             for k in range(i):
                 rows[i] = rows[i] - unit[i, k] * rows[k]
-                ones[i] = ones[i] - unit[i, k] * ones[k]
-        out = ones[0] * lax.rsqrt(entry[0, 0])
+        out = rows[0] * lax.rsqrt(entry[0, 0])
         for i in range(1, 8):
-            out = jnp.where(sublane == i, ones[i] * lax.rsqrt(entry[i, i]), out)
-        done.append(out)
+            out = jnp.where(sublane == i, rows[i] * lax.rsqrt(entry[i, i]), out)
+        done.append(jnp.where(lane < base + 8, out, 0.0))
         if p == count - 1:
             break
         for i in reversed(range(8)):
             rows[i] = rows[i] * inverse[i]
-            ones[i] = ones[i] * inverse[i]
-            for k in range(i + 1, 8):
+            for k in reversed(range(i + 1, 8)):
                 rows[i] = rows[i] - unit[k, i] * rows[k]
-                ones[i] = ones[i] - unit[k, i] * ones[k]
         for q in range(p + 1, count):
-            columns = [spread_column(left[q], base + i) for i in range(8)]
-            for i in range(8):
-                left[q] = left[q] - columns[i] * rows[i]
-                right[q] = right[q] - columns[i] * ones[i]
+            columns = [spread_column(blocks[q], base + i) for i in range(8)]
+            blocks[q] = jnp.where(own, 0.0, blocks[q])
+            for i in reversed(range(8)):
+                blocks[q] = blocks[q] - columns[i] * rows[i]
     return jnp.concatenate(done, axis=0)
 
 
@@ -407,10 +404,10 @@
         pair = pair_ref[...]
         lower = dot_t(row_ref[:, : 2 * bands] * scale, pair, HIGH)
         last = inverse_factor(row_ref[:, 2 * bands :] * scale - dot_t(lower, lower, HIGH))
+        first, through = dot(turned_ref[:, : 2 * bands], pair, HIGH), dot(lower, pair, HIGH)
         tail = dot(turned_ref[:, 2 * bands :], last, HIGH)
         c_ref[:, 2 * bands :] = tail
-        rest = turned_ref[:, : 2 * bands] - dot(tail, lower, HIGH)
-        c_ref[:, : 2 * bands] = dot(rest, pair, HIGH)
+        c_ref[:, : 2 * bands] = first - dot(tail, through, HIGH)
 
     here = pl.ds(pl.multiple_of(step * count, count), count)
     for to_ref, sem in ((parts_ref, sems.at[0, step]), (both_ref, sems.at[1, step])):

time: 636 us -> 635 us (level)
  transfers between devices with their start and end apart: 25 -> 25, of which waited for: 22 -> 22; matrix products, arithmetic and copies ran while one was open for 4% -> 4% of each run, Pallas kernels for 15% -> 14%
where the time goes in v4:
time: 635 us; the launch traced here: 634 us
  waiting for transfers between devices  436 us (69%)
  Pallas kernels  115 us (18%)
  starting transfers between devices  43.6 us (7%)
  local copies, waits for them, and re-layouts  27.9 us (4%)
  other arithmetic  10.3 us (2%)
    ppermute x5, waiting for transfers between devices, butterfly_sum(): lax.ppermute(value, axis, [(i, i ^ step) for i in range(devices)])  157 us
    ppermute x4, waiting for transfers between devices, half_of_sum(): lax.ppermute(mine, axis, [(i, i ^ step) for i in range(devices)])  91.3 us
    all_to_all x4, waiting for transfers between devices, exchange(): got = lax.all_to_all(blocks, 'grid', 0, 0, tiled=True)  77 us
    ppermute x2, waiting for transfers between devices, halos(): return (lax.ppermute(last, axis, up), lax.ppermute(first, axis, down))  69.8 us
    pallas_call x1, Pallas kernels, kinetic(): pl.pallas_call(functools.partial(kinetic_kernel, weights), grid=(bands,),...  48.1 us
    ppermute x6, waiting for transfers between devices, half_of_sum(): lax.ppermute(mine, ('band', 'grid'), [(i, i ^ f) for i in range(bands * g...  35.9 us
    all_to_all x4, starting transfers between devices, exchange(): got = lax.all_to_all(blocks, 'grid', 0, 0, tiled=True)  21 us
    pallas_call x1, Pallas kernels, finish(): pl.pallas_call(functools.partial(finish_kernel, scale), grid=(planes // S...  19.5 us
  transfers between devices with their start and end apart: 25, of which 22 were waited for; matrix products, arithmetic and copies ran while one was open for 4% of the time, Pallas kernels for 14%

profile of v4, /device:TPU:0, one launch (start us, length us, event | category | flops | bytes accessed | tf_op | source)
XLA Modules:
  0.0 634.0 jit_solution(7703956738346311406)
XLA Ops:
  0.0 7.8 %copy_bitcast_fusion = f32[8,16,16,8,128]{4,3,2,1,0:T(8,128)} fusion(f32[16,16,64,128]{3,2,1,0:T(8,128)} %w_ref.1), kind=kLoop, calls=%fused_computation | loop fusion | bytes 16777216 | tf_op jit(solution)/shard_map/transpose | solution.py:455
  7.8 7.3 %all-to-all-start = ((f32[8,16,16,8,128]{4,3,2,1,0:T(8,128)}), f32[8,16,16,8,128]{4,3,2,1,0:T(8,128)}, u32[]{:S(2)}, u32[]{:S(2)}) async-start(f32[8,16,16,8,128]{4,3,2,1,0:T(8,128)} %copy_bitcast_fusion), calls=%async_computation | async-start | bytes 16777216 | tf_op jit(solution)/shard_map/all_to_all | solution.py:458
  19.8 68.2 %collective-permute-done.1.hi_ref = f32[16,6,64,128]{3,2,1,0:T(8,128)S(1)} collective-permute-done((f32[16,6,64,128]{3,2,1,0:T(8,128)S(1)}, f32[16,6,64,128]{3,2,1,0:T(8,128)S(1)}, u32[]{:S(2)}, u32[]{:S(2)}) %collective-permute-start.1) | collective-permute-done | bytes 3145760 | tf_op jit(solution)/shard_map/ppermute | solution.py:32
  89.6 48.1 %kinetic.1 = (f32[8,16,16,8,128]{4,3,2,1,0:T(8,128)S(1)}, f32[16,8,128]{2,1,0:T(8,128)S(1)}) custom-call(f32[16,16,64,128]{3,2,1,0:T(8,128)} %w_ref.1, f32[16,6,64,128]{3,2,1,0:T(8,128)S(1)} %collective-permute-done.lo_ref, f32[16,6,64,128]{3,2,1,0:T(8,128)S(1)} %collective-permute-done.1.hi_ref), custom_call_target="tpu_custom_call" | custom-call | flops 125829120 | bytes 23068672 | tf_op jit(solution)/shard_map/kinetic/pallas_call | solution.py:106
  141.0 57.2 %all-to-all-done = f32[8,16,16,8,128]{4,3,2,1,0:T(8,128)} async-done(((f32[8,16,16,8,128]{4,3,2,1,0:T(8,128)}), f32[8,16,16,8,128]{4,3,2,1,0:T(8,128)}, u32[]{:S(2)}, u32[]{:S(2)}) %all-to-all-start) | async-done | bytes 8388640 | tf_op jit(solution)/shard_map/all_to_all | solution.py:458
  198.2 5.1 all-to-all-start.1
  203.6 5.1 multiply_reduce_fusion
  216.0 54.3 %collective-permute-done.4 = f32[2,128]{1,0:T(2,128)S(1)} collective-permute-done((f32[2,128]{1,0:T(2,128)S(1)}, f32[2,128]{1,0:T(2,128)S(1)}, u32[]{:S(2)}, u32[]{:S(2)}) %collective-permute-start.4) | collective-permute-done | bytes 1056 | tf_op jit(solution)/shard_map/ppermute | solution.py:39
  271.8 6.2 copy_bitcast_fusion.1
  278.1 60.2 %collective-permute-done.5 = f32[2,128]{1,0:T(2,128)S(1)} collective-permute-done((f32[2,128]{1,0:T(2,128)S(1)}, f32[2,128]{1,0:T(2,128)S(1)}, u32[]{:S(2)}, u32[]{:S(2)}) %collective-permute-start.5) | collective-permute-done | bytes 1056 | tf_op jit(solution)/shard_map/ppermute | solution.py:39
  346.2 39.4 %collective-permute-done.6 = f32[2,128]{1,0:T(2,128)S(1)} collective-permute-done((f32[2,128]{1,0:T(2,128)S(1)}, f32[2,128]{1,0:T(2,128)S(1)}, u32[]{:S(2)}, u32[]{:S(2)}) %collective-permute-start.6) | collective-permute-done | bytes 1056 | tf_op jit(solution)/shard_map/ppermute | solution.py:39
  385.6 4.8 all-to-all-start.3
  391.1 17.9 %gram_pair.1 = (f32[256,256]{1,0:T(8,128)}, bf16[512,16384]{1,0:T(8,128)(2,1)}) custom-call(f32[128,16,8,128]{3,2,1,0:T(8,128)} %bitcast.8.t_ref, f32[128,16,8,128]{3,2,1,0:T(8,128)} %bitcast.9.w_ref, f32[16,8,128]{2,1,0:T(8,128)} %v_ref.1, f32[128,128]{1,0:T(8,128)} %broadcast_in_dim.2.ritz_ref), custom_call_target="tpu_custom_call" | custom-call | flops 4294967296 | bytes 33554432 | tf_op jit(solution)/shard_map/gram_pair/pallas_call | solution.py:246
  416.0 29.8 %collective-permute-done.10 = f32[128,256]{1,0:T(8,128)S(1)} collective-permute-done((f32[128,256]{1,0:T(8,128)S(1)}, f32[128,256]{1,0:T(8,128)S(1)}, u32[]{:S(2)}, u32[]{:S(2)}) %collective-permute-start.10) | collective-permute-done | bytes 131104 | tf_op jit(solution)/shard_map/ppermute | solution.py:58
  447.6 46.6 %collective-permute-done.11 = f32[128,256]{1,0:T(8,128)S(1)} collective-permute-done((f32[128,256]{1,0:T(8,128)S(1)}, f32[128,256]{1,0:T(8,128)S(1)}, u32[]{:S(2)}, u32[]{:S(2)}) %collective-permute-start.11) | collective-permute-done | bytes 131104 | tf_op jit(solution)/shard_map/ppermute | solution.py:65
  498.3 34.8 %collective-permute-done.12 = f32[128,256]{1,0:T(8,128)S(1)} collective-permute-done((f32[128,256]{1,0:T(8,128)S(1)}, f32[128,256]{1,0:T(8,128)S(1)}, u32[]{:S(2)}, u32[]{:S(2)}) %collective-permute-start.12) | collective-permute-done | bytes 131104 | tf_op jit(solution)/shard_map/ppermute | solution.py:65
  539.1 5.7 factor_first.1.first_ref
  544.8 7.0 %factor_second.1.pair_ref = f32[256,256]{1,0:T(8,128)} custom-call(f32[256,256]{1,0:T(8,128)} %pad_maximum_fusion.g_ref, f32[128,128]{1,0:T(8,128)} %factor_first.1.first_ref), custom_call_target="tpu_custom_call" | custom-call | flops 1000000000 | bytes 262144 | tf_op jit(solution)/shard_map/factor_second/pallas_call | solution.py:376
  551.7 12.4 %gram_row.2 = (f32[256,768]{1,0:T(8,128)}, bf16[256,12288]{1,0:T(8,128)(2,1)}) custom-call(bf16[512,16384]{1,0:T(8,128)(2,1)} %get-tuple-element.28.parts_ref.parts_hbm, f32[128,12,8,128]{3,2,1,0:T(8,128)} %bitcast.12.d_ref), custom_call_target="tpu_custom_call" | custom-call | flops 3623878656 | bytes 18874368 | tf_op jit(solution)/shard_map/gram_row/pallas_call | solution.py:268
  565.4 19.8 %all-to-all-done.2 = f32[8,16,4,8,128]{4,3,2,1,0:T(8,128)S(1)} async-done(((f32[8,16,4,8,128]{4,3,2,1,0:T(8,128)}), f32[8,16,4,8,128]{4,3,2,1,0:T(8,128)S(1)}, u32[]{:S(2)}, u32[]{:S(2)}) %all-to-all-start.2) | async-done | bytes 2097184 | tf_op jit(solution)/shard_map/all_to_all | solution.py:458
  585.2 4.9 gram_row.3
  601.1 4.6 collective-permute-done.18
  606.9 5.3 collective-permute-done.19
  614.3 19.5 %finish.1 = f32[128,16,8,128]{3,2,1,0:T(8,128)} custom-call(f32[128,384]{1,0:T(8,128)} %pad_maximum_fusion.2.row_ref, f32[256,256]{1,0:T(8,128)} %factor_second.1.pair_ref, f32[128,384]{1,0:T(8,128)} %bitcast.25, bf16[512,16384]{1,0:T(8,128)(2,1)} %get-tuple-element.28.parts_ref.parts_hbm, bf16[256,12288]{1,0:T(8,128)(2,1)} %get-tuple-element.37.early_hbm, ...), custom_call_target="tpu_custom_call" | custom-call | flops 4831838208 | bytes 33554432 | tf_op jit(solution)/shard_map/finish/pallas_call | solution.py:423
  (83 shorter events, 61.6 us)
Async XLA Ops:
  7.8 190.4 %all-to-all-start = ((f32[8,16,16,8,128]{4,3,2,1,0:T(8,128)}), f32[8,16,16,8,128]{4,3,2,1,0:T(8,128)}, u32[]{:S(2)}, u32[]{:S(2)}) async-start(f32[8,16,16,8,128]{4,3,2,1,0:T(8,128)} %copy_bitcast_fusion), calls=%async_computation | async-start | bytes 16777216 | tf_op jit(solution)/shard_map/all_to_all | solution.py:458
  19.0 68.9 %collective-permute-start.1 = (f32[16,6,64,128]{3,2,1,0:T(8,128)S(1)}, f32[16,6,64,128]{3,2,1,0:T(8,128)S(1)}, u32[]{:S(2)}, u32[]{:S(2)}) collective-permute-start(f32[16,6,64,128]{3,2,1,0:T(8,128)S(1)} %get-tuple-element.41), channel_id=1, source_target_pairs={{8,0},{16,8},{24,16},{0,24},{9,1},{17,9},{25,17},{1,25},{10,2},{18... | collective-permute-start | bytes 9437192 | tf_op jit(solution)/shard_map/ppermute | solution.py:32
  19.8 69.8 %collective-permute-start = (f32[16,6,64,128]{3,2,1,0:T(8,128)S(1)}, f32[16,6,64,128]{3,2,1,0:T(8,128)S(1)}, u32[]{:S(2)}, u32[]{:S(2)}) collective-permute-start(f32[16,6,64,128]{3,2,1,0:T(8,128)S(1)} %get-tuple-element.42), channel_id=1, source_target_pairs={{0,8},{8,16},{16,24},{24,0},{1,9},{9,17},{17,25},{25,1},{2,10},{10... | collective-permute-start | bytes 9437192 | tf_op jit(solution)/shard_map/ppermute | solution.py:32
  198.2 187.4 %all-to-all-start.1 = ((f32[8,16,16,8,128]{4,3,2,1,0:T(8,128)}), f32[8,16,16,8,128]{4,3,2,1,0:T(8,128)}, u32[]{:S(2)}, u32[]{:S(2)}) async-start(f32[8,16,16,8,128]{4,3,2,1,0:T(8,128)} %copy-done), calls=%async_computation.1 | async-start | bytes 16777216 | tf_op jit(solution)/shard_map/all_to_all | solution.py:458
  210.3 3.6 collective-permute-start.3
  213.9 56.4 %collective-permute-start.4 = (f32[2,128]{1,0:T(2,128)S(1)}, f32[2,128]{1,0:T(2,128)S(1)}, u32[]{:S(2)}, u32[]{:S(2)}) collective-permute-start(f32[2,128]{1,0:T(2,128)S(1)} %fusion.3), channel_id=1, source_target_pairs={{0,1},{1,0},{2,3},{3,2},{4,5},{5,4},{6,7},{7,6},{8,9},{9,8},{10,11... | collective-permute-start | bytes 3080 | tf_op jit(solution)/shard_map/ppermute | solution.py:39
  270.3 67.9 %collective-permute-start.5 = (f32[2,128]{1,0:T(2,128)S(1)}, f32[2,128]{1,0:T(2,128)S(1)}, u32[]{:S(2)}, u32[]{:S(2)}) collective-permute-start(f32[2,128]{1,0:T(2,128)S(1)} %add.91), channel_id=1, source_target_pairs={{0,2},{1,3},{2,0},{3,1},{4,6},{5,7},{6,4},{7,5},{8,10},{9,11},{10,... | collective-permute-start | bytes 3080 | tf_op jit(solution)/shard_map/ppermute | solution.py:39
  338.3 47.3 %collective-permute-start.6 = (f32[2,128]{1,0:T(2,128)S(1)}, f32[2,128]{1,0:T(2,128)S(1)}, u32[]{:S(2)}, u32[]{:S(2)}) collective-permute-start(f32[2,128]{1,0:T(2,128)S(1)} %add.92), channel_id=1, source_target_pairs={{0,4},{1,5},{2,6},{3,7},{4,0},{5,1},{6,2},{7,3},{8,12},{9,13},{10,... | collective-permute-start | bytes 3080 | tf_op jit(solution)/shard_map/ppermute | solution.py:39
  385.6 147.5 %all-to-all-start.3 = ((f32[8,16,12,8,128]{4,3,2,1,0:T(8,128)}), f32[8,16,12,8,128]{4,3,2,1,0:T(8,128)}, u32[]{:S(2)}, u32[]{:S(2)}) async-start(f32[8,16,12,8,128]{4,3,2,1,0:T(8,128)} %copy_bitcast_fusion.1), calls=%async_computation.3 | async-start | bytes 12582912 | tf_op jit(solution)/shard_map/all_to_all | solution.py:458
  410.0 1.4 collective-permute-start.7
  412.5 33.4 %collective-permute-start.10 = (f32[128,256]{1,0:T(8,128)S(1)}, f32[128,256]{1,0:T(8,128)S(1)}, u32[]{:S(2)}, u32[]{:S(2)}) collective-permute-start(f32[128,256]{1,0:T(8,128)S(1)} %select_add_fusion), channel_id=1, source_target_pairs={{0,17},{1,16},{2,19},{3,18},{4,21},{5,20},{6,23},{7,22},{8,25},{9,... | collective-permute-start | bytes 393224 | tf_op jit(solution)/shard_map/ppermute | solution.py:58
  415.4 30.5 %collective-permute-start.9 = (f32[128,256]{1,0:T(8,128)S(1)}, f32[128,256]{1,0:T(8,128)S(1)}, u32[]{:S(2)}, u32[]{:S(2)}) collective-permute-start(f32[128,256]{1,0:T(8,128)S(1)} %select_add_fusion), channel_id=1, source_target_pairs={{0,16},{1,17},{2,18},{3,19},{4,20},{5,21},{6,22},{7,23},{8,24},{9,... | collective-permute-start | bytes 393224 | tf_op jit(solution)/shard_map/ppermute | solution.py:58
  415.9 31.6 %collective-permute-start.8 = (f32[128,256]{1,0:T(8,128)S(1)}, f32[128,256]{1,0:T(8,128)S(1)}, u32[]{:S(2)}, u32[]{:S(2)}) collective-permute-start(f32[128,256]{1,0:T(8,128)S(1)} %select_add_fusion), channel_id=1, source_target_pairs={{0,1},{1,0},{2,3},{3,2},{4,5},{5,4},{6,7},{7,6},{8,9},{9,8},{10,11... | collective-permute-start | bytes 393224 | tf_op jit(solution)/shard_map/ppermute | solution.py:58
  447.5 46.7 %collective-permute-start.11 = (f32[128,256]{1,0:T(8,128)S(1)}, f32[128,256]{1,0:T(8,128)S(1)}, u32[]{:S(2)}, u32[]{:S(2)}) collective-permute-start(f32[128,256]{1,0:T(8,128)S(1)} %add_add_fusion), channel_id=1, source_target_pairs={{0,2},{1,3},{2,0},{3,1},{4,6},{5,7},{6,4},{7,5},{8,10},{9,11},{10,... | collective-permute-start | bytes 393224 | tf_op jit(solution)/shard_map/ppermute | solution.py:65
  494.2 38.9 %collective-permute-start.12 = (f32[128,256]{1,0:T(8,128)S(1)}, f32[128,256]{1,0:T(8,128)S(1)}, u32[]{:S(2)}, u32[]{:S(2)}) collective-permute-start(f32[128,256]{1,0:T(8,128)S(1)} %add.98), channel_id=1, source_target_pairs={{0,4},{1,5},{2,6},{3,7},{4,0},{5,1},{6,2},{7,3},{8,12},{9,13},{10,... | collective-permute-start | bytes 393224 | tf_op jit(solution)/shard_map/ppermute | solution.py:65
  533.1 52.1 %all-to-all-start.2 = ((f32[8,16,4,8,128]{4,3,2,1,0:T(8,128)}), f32[8,16,4,8,128]{4,3,2,1,0:T(8,128)S(1)}, u32[]{:S(2)}, u32[]{:S(2)}) async-start(f32[8,16,4,8,128]{4,3,2,1,0:T(8,128)} %copy_bitcast_fusion.2), calls=%async_computation.2 | async-start | bytes 4194304 | tf_op jit(solution)/shard_map/all_to_all | solution.py:458
  536.9 1.4 collective-permute-start.13
  591.6 1.4 collective-permute-start.14
  593.0 5.9 collective-permute-start.17
  595.5 5.5 collective-permute-start.16
  596.0 5.0 collective-permute-start.15
  601.0 4.7 collective-permute-start.18
  605.7 6.5 %collective-permute-start.19 = (f32[64,384]{1,0:T(8,128)S(1)}, f32[64,384]{1,0:T(8,128)S(1)}, u32[]{:S(2)}, u32[]{:S(2)}) collective-permute-start(f32[64,384]{1,0:T(8,128)S(1)} %add.111), channel_id=1, source_target_pairs={{0,4},{1,5},{2,6},{3,7},{4,0},{5,1},{6,2},{7,3},{8,12},{9,13},{10,... | collective-permute-start | bytes 294920 | tf_op jit(solution)/shard_map/ppermute | solution.py:65
  612.2 1.4 collective-permute-start.20
  (5 other events, 86.4 us)

commit v5 on v4

--- a/solution.py
+++ b/solution.py
@@ -403,8 +403,9 @@
             pltpu.make_async_copy(own, both_ref.at[:, to], sems.at[1, i]).start()
         pair = pair_ref[...]
         lower = dot_t(row_ref[:, : 2 * bands] * scale, pair, HIGH)
-        last = inverse_factor(row_ref[:, 2 * bands :] * scale - dot_t(lower, lower, HIGH))
+        rest = row_ref[:, 2 * bands :] * scale - dot_t(lower, lower, HIGH)
         first, through = dot(turned_ref[:, : 2 * bands], pair, HIGH), dot(lower, pair, HIGH)
+        last = inverse_factor(rest)
         tail = dot(turned_ref[:, 2 * bands :], last, HIGH)
         c_ref[:, 2 * bands :] = tail
         c_ref[:, : 2 * bands] = first - dot(tail, through, HIGH)

time: 635 us -> 635 us (level)
  no operation moved by 1% of the time
where the time goes in v5:
time: 635 us; the launch traced here: 634 us
  waiting for transfers between devices  436 us (69%)
  Pallas kernels  115 us (18%)
  starting transfers between devices  43.6 us (7%)
  local copies, waits for them, and re-layouts  27.9 us (4%)
  other arithmetic  10.3 us (2%)
    ppermute x5, waiting for transfers between devices, butterfly_sum(): lax.ppermute(value, axis, [(i, i ^ step) for i in range(devices)])  157 us
    ppermute x4, waiting for transfers between devices, half_of_sum(): lax.ppermute(mine, axis, [(i, i ^ step) for i in range(devices)])  91.3 us
    all_to_all x4, waiting for transfers between devices, exchange(): got = lax.all_to_all(blocks, 'grid', 0, 0, tiled=True)  77 us
    ppermute x2, waiting for transfers between devices, halos(): return (lax.ppermute(last, axis, up), lax.ppermute(first, axis, down))  69.8 us
    pallas_call x1, Pallas kernels, kinetic(): pl.pallas_call(functools.partial(kinetic_kernel, weights), grid=(bands,),...  48.1 us
    ppermute x6, waiting for transfers between devices, half_of_sum(): lax.ppermute(mine, ('band', 'grid'), [(i, i ^ f) for i in range(bands * g...  35.9 us
    all_to_all x4, starting transfers between devices, exchange(): got = lax.all_to_all(blocks, 'grid', 0, 0, tiled=True)  21 us
    pallas_call x1, Pallas kernels, finish(): pl.pallas_call(functools.partial(finish_kernel, scale), grid=(planes // S...  19.5 us
  transfers between devices with their start and end apart: 25, of which 22 were waited for; matrix products, arithmetic and copies ran while one was open for 4% of the time, Pallas kernels for 14%

profile of v5, /device:TPU:0, one launch (start us, length us, event | category | flops | bytes accessed | tf_op | source)
XLA Modules:
  0.0 634.0 jit_solution(4161907795291474972)
XLA Ops:
  0.0 7.8 %copy_bitcast_fusion = f32[8,16,16,8,128]{4,3,2,1,0:T(8,128)} fusion(f32[16,16,64,128]{3,2,1,0:T(8,128)} %w_ref.1), kind=kLoop, calls=%fused_computation | loop fusion | bytes 16777216 | tf_op jit(solution)/shard_map/transpose | solution.py:456
  7.8 7.3 %all-to-all-start = ((f32[8,16,16,8,128]{4,3,2,1,0:T(8,128)}), f32[8,16,16,8,128]{4,3,2,1,0:T(8,128)}, u32[]{:S(2)}, u32[]{:S(2)}) async-start(f32[8,16,16,8,128]{4,3,2,1,0:T(8,128)} %copy_bitcast_fusion), calls=%async_computation | async-start | bytes 16777216 | tf_op jit(solution)/shard_map/all_to_all | solution.py:459
  19.8 68.2 %collective-permute-done.1.hi_ref = f32[16,6,64,128]{3,2,1,0:T(8,128)S(1)} collective-permute-done((f32[16,6,64,128]{3,2,1,0:T(8,128)S(1)}, f32[16,6,64,128]{3,2,1,0:T(8,128)S(1)}, u32[]{:S(2)}, u32[]{:S(2)}) %collective-permute-start.1) | collective-permute-done | bytes 3145760 | tf_op jit(solution)/shard_map/ppermute | solution.py:32
  89.6 48.1 %kinetic.1 = (f32[8,16,16,8,128]{4,3,2,1,0:T(8,128)S(1)}, f32[16,8,128]{2,1,0:T(8,128)S(1)}) custom-call(f32[16,16,64,128]{3,2,1,0:T(8,128)} %w_ref.1, f32[16,6,64,128]{3,2,1,0:T(8,128)S(1)} %collective-permute-done.lo_ref, f32[16,6,64,128]{3,2,1,0:T(8,128)S(1)} %collective-permute-done.1.hi_ref), custom_call_target="tpu_custom_call" | custom-call | flops 125829120 | bytes 23068672 | tf_op jit(solution)/shard_map/kinetic/pallas_call | solution.py:106
  141.0 57.2 %all-to-all-done = f32[8,16,16,8,128]{4,3,2,1,0:T(8,128)} async-done(((f32[8,16,16,8,128]{4,3,2,1,0:T(8,128)}), f32[8,16,16,8,128]{4,3,2,1,0:T(8,128)}, u32[]{:S(2)}, u32[]{:S(2)}) %all-to-all-start) | async-done | bytes 8388640 | tf_op jit(solution)/shard_map/all_to_all | solution.py:459
  198.2 5.1 all-to-all-start.1
  203.6 5.1 multiply_reduce_fusion
  216.0 54.3 %collective-permute-done.4 = f32[2,128]{1,0:T(2,128)S(1)} collective-permute-done((f32[2,128]{1,0:T(2,128)S(1)}, f32[2,128]{1,0:T(2,128)S(1)}, u32[]{:S(2)}, u32[]{:S(2)}) %collective-permute-start.4) | collective-permute-done | bytes 1056 | tf_op jit(solution)/shard_map/ppermute | solution.py:39
  271.8 6.2 copy_bitcast_fusion.1
  278.1 60.2 %collective-permute-done.5 = f32[2,128]{1,0:T(2,128)S(1)} collective-permute-done((f32[2,128]{1,0:T(2,128)S(1)}, f32[2,128]{1,0:T(2,128)S(1)}, u32[]{:S(2)}, u32[]{:S(2)}) %collective-permute-start.5) | collective-permute-done | bytes 1056 | tf_op jit(solution)/shard_map/ppermute | solution.py:39
  346.2 39.4 %collective-permute-done.6 = f32[2,128]{1,0:T(2,128)S(1)} collective-permute-done((f32[2,128]{1,0:T(2,128)S(1)}, f32[2,128]{1,0:T(2,128)S(1)}, u32[]{:S(2)}, u32[]{:S(2)}) %collective-permute-start.6) | collective-permute-done | bytes 1056 | tf_op jit(solution)/shard_map/ppermute | solution.py:39
  385.6 4.8 all-to-all-start.3
  391.1 17.9 %gram_pair.1 = (f32[256,256]{1,0:T(8,128)}, bf16[512,16384]{1,0:T(8,128)(2,1)}) custom-call(f32[128,16,8,128]{3,2,1,0:T(8,128)} %bitcast.8.t_ref, f32[128,16,8,128]{3,2,1,0:T(8,128)} %bitcast.9.w_ref, f32[16,8,128]{2,1,0:T(8,128)} %v_ref.1, f32[128,128]{1,0:T(8,128)} %broadcast_in_dim.2.ritz_ref), custom_call_target="tpu_custom_call" | custom-call | flops 4294967296 | bytes 33554432 | tf_op jit(solution)/shard_map/gram_pair/pallas_call | solution.py:246
  416.0 29.8 %collective-permute-done.10 = f32[128,256]{1,0:T(8,128)S(1)} collective-permute-done((f32[128,256]{1,0:T(8,128)S(1)}, f32[128,256]{1,0:T(8,128)S(1)}, u32[]{:S(2)}, u32[]{:S(2)}) %collective-permute-start.10) | collective-permute-done | bytes 131104 | tf_op jit(solution)/shard_map/ppermute | solution.py:58
  447.6 46.6 %collective-permute-done.11 = f32[128,256]{1,0:T(8,128)S(1)} collective-permute-done((f32[128,256]{1,0:T(8,128)S(1)}, f32[128,256]{1,0:T(8,128)S(1)}, u32[]{:S(2)}, u32[]{:S(2)}) %collective-permute-start.11) | collective-permute-done | bytes 131104 | tf_op jit(solution)/shard_map/ppermute | solution.py:65
  498.3 34.8 %collective-permute-done.12 = f32[128,256]{1,0:T(8,128)S(1)} collective-permute-done((f32[128,256]{1,0:T(8,128)S(1)}, f32[128,256]{1,0:T(8,128)S(1)}, u32[]{:S(2)}, u32[]{:S(2)}) %collective-permute-start.12) | collective-permute-done | bytes 131104 | tf_op jit(solution)/shard_map/ppermute | solution.py:65
  539.1 5.7 factor_first.1.first_ref
  544.8 7.0 %factor_second.1.pair_ref = f32[256,256]{1,0:T(8,128)} custom-call(f32[256,256]{1,0:T(8,128)} %pad_maximum_fusion.g_ref, f32[128,128]{1,0:T(8,128)} %factor_first.1.first_ref), custom_call_target="tpu_custom_call" | custom-call | flops 1000000000 | bytes 262144 | tf_op jit(solution)/shard_map/factor_second/pallas_call | solution.py:376
  551.7 12.4 %gram_row.2 = (f32[256,768]{1,0:T(8,128)}, bf16[256,12288]{1,0:T(8,128)(2,1)}) custom-call(bf16[512,16384]{1,0:T(8,128)(2,1)} %get-tuple-element.28.parts_ref.parts_hbm, f32[128,12,8,128]{3,2,1,0:T(8,128)} %bitcast.12.d_ref), custom_call_target="tpu_custom_call" | custom-call | flops 3623878656 | bytes 18874368 | tf_op jit(solution)/shard_map/gram_row/pallas_call | solution.py:268
  565.4 19.8 %all-to-all-done.2 = f32[8,16,4,8,128]{4,3,2,1,0:T(8,128)S(1)} async-done(((f32[8,16,4,8,128]{4,3,2,1,0:T(8,128)}), f32[8,16,4,8,128]{4,3,2,1,0:T(8,128)S(1)}, u32[]{:S(2)}, u32[]{:S(2)}) %all-to-all-start.2) | async-done | bytes 2097184 | tf_op jit(solution)/shard_map/all_to_all | solution.py:459
  585.2 4.9 gram_row.3
  601.1 4.6 collective-permute-done.18
  606.9 5.3 collective-permute-done.19
  614.3 19.5 %finish.1 = f32[128,16,8,128]{3,2,1,0:T(8,128)} custom-call(f32[128,384]{1,0:T(8,128)} %pad_maximum_fusion.2.row_ref, f32[256,256]{1,0:T(8,128)} %factor_second.1.pair_ref, f32[128,384]{1,0:T(8,128)} %bitcast.25, bf16[512,16384]{1,0:T(8,128)(2,1)} %get-tuple-element.28.parts_ref.parts_hbm, bf16[256,12288]{1,0:T(8,128)(2,1)} %get-tuple-element.37.early_hbm, ...), custom_call_target="tpu_custom_call" | custom-call | flops 4831838208 | bytes 33554432 | tf_op jit(solution)/shard_map/finish/pallas_call | solution.py:424
  (83 shorter events, 61.6 us)
Async XLA Ops:
  7.8 190.4 %all-to-all-start = ((f32[8,16,16,8,128]{4,3,2,1,0:T(8,128)}), f32[8,16,16,8,128]{4,3,2,1,0:T(8,128)}, u32[]{:S(2)}, u32[]{:S(2)}) async-start(f32[8,16,16,8,128]{4,3,2,1,0:T(8,128)} %copy_bitcast_fusion), calls=%async_computation | async-start | bytes 16777216 | tf_op jit(solution)/shard_map/all_to_all | solution.py:459
  19.0 68.9 %collective-permute-start.1 = (f32[16,6,64,128]{3,2,1,0:T(8,128)S(1)}, f32[16,6,64,128]{3,2,1,0:T(8,128)S(1)}, u32[]{:S(2)}, u32[]{:S(2)}) collective-permute-start(f32[16,6,64,128]{3,2,1,0:T(8,128)S(1)} %get-tuple-element.41), channel_id=1, source_target_pairs={{8,0},{16,8},{24,16},{0,24},{9,1},{17,9},{25,17},{1,25},{10,2},{18... | collective-permute-start | bytes 9437192 | tf_op jit(solution)/shard_map/ppermute | solution.py:32
  19.8 69.8 %collective-permute-start = (f32[16,6,64,128]{3,2,1,0:T(8,128)S(1)}, f32[16,6,64,128]{3,2,1,0:T(8,128)S(1)}, u32[]{:S(2)}, u32[]{:S(2)}) collective-permute-start(f32[16,6,64,128]{3,2,1,0:T(8,128)S(1)} %get-tuple-element.42), channel_id=1, source_target_pairs={{0,8},{8,16},{16,24},{24,0},{1,9},{9,17},{17,25},{25,1},{2,10},{10... | collective-permute-start | bytes 9437192 | tf_op jit(solution)/shard_map/ppermute | solution.py:32
  198.2 187.4 %all-to-all-start.1 = ((f32[8,16,16,8,128]{4,3,2,1,0:T(8,128)}), f32[8,16,16,8,128]{4,3,2,1,0:T(8,128)}, u32[]{:S(2)}, u32[]{:S(2)}) async-start(f32[8,16,16,8,128]{4,3,2,1,0:T(8,128)} %copy-done), calls=%async_computation.1 | async-start | bytes 16777216 | tf_op jit(solution)/shard_map/all_to_all | solution.py:459
  210.3 3.6 collective-permute-start.3
  213.9 56.4 %collective-permute-start.4 = (f32[2,128]{1,0:T(2,128)S(1)}, f32[2,128]{1,0:T(2,128)S(1)}, u32[]{:S(2)}, u32[]{:S(2)}) collective-permute-start(f32[2,128]{1,0:T(2,128)S(1)} %fusion.3), channel_id=1, source_target_pairs={{0,1},{1,0},{2,3},{3,2},{4,5},{5,4},{6,7},{7,6},{8,9},{9,8},{10,11... | collective-permute-start | bytes 3080 | tf_op jit(solution)/shard_map/ppermute | solution.py:39
  270.3 67.9 %collective-permute-start.5 = (f32[2,128]{1,0:T(2,128)S(1)}, f32[2,128]{1,0:T(2,128)S(1)}, u32[]{:S(2)}, u32[]{:S(2)}) collective-permute-start(f32[2,128]{1,0:T(2,128)S(1)} %add.91), channel_id=1, source_target_pairs={{0,2},{1,3},{2,0},{3,1},{4,6},{5,7},{6,4},{7,5},{8,10},{9,11},{10,... | collective-permute-start | bytes 3080 | tf_op jit(solution)/shard_map/ppermute | solution.py:39
  338.3 47.3 %collective-permute-start.6 = (f32[2,128]{1,0:T(2,128)S(1)}, f32[2,128]{1,0:T(2,128)S(1)}, u32[]{:S(2)}, u32[]{:S(2)}) collective-permute-start(f32[2,128]{1,0:T(2,128)S(1)} %add.92), channel_id=1, source_target_pairs={{0,4},{1,5},{2,6},{3,7},{4,0},{5,1},{6,2},{7,3},{8,12},{9,13},{10,... | collective-permute-start | bytes 3080 | tf_op jit(solution)/shard_map/ppermute | solution.py:39
  385.6 147.5 %all-to-all-start.3 = ((f32[8,16,12,8,128]{4,3,2,1,0:T(8,128)}), f32[8,16,12,8,128]{4,3,2,1,0:T(8,128)}, u32[]{:S(2)}, u32[]{:S(2)}) async-start(f32[8,16,12,8,128]{4,3,2,1,0:T(8,128)} %copy_bitcast_fusion.1), calls=%async_computation.3 | async-start | bytes 12582912 | tf_op jit(solution)/shard_map/all_to_all | solution.py:459
  410.0 1.4 collective-permute-start.7
  412.5 33.4 %collective-permute-start.10 = (f32[128,256]{1,0:T(8,128)S(1)}, f32[128,256]{1,0:T(8,128)S(1)}, u32[]{:S(2)}, u32[]{:S(2)}) collective-permute-start(f32[128,256]{1,0:T(8,128)S(1)} %select_add_fusion), channel_id=1, source_target_pairs={{0,17},{1,16},{2,19},{3,18},{4,21},{5,20},{6,23},{7,22},{8,25},{9,... | collective-permute-start | bytes 393224 | tf_op jit(solution)/shard_map/ppermute | solution.py:58
  415.4 30.5 %collective-permute-start.9 = (f32[128,256]{1,0:T(8,128)S(1)}, f32[128,256]{1,0:T(8,128)S(1)}, u32[]{:S(2)}, u32[]{:S(2)}) collective-permute-start(f32[128,256]{1,0:T(8,128)S(1)} %select_add_fusion), channel_id=1, source_target_pairs={{0,16},{1,17},{2,18},{3,19},{4,20},{5,21},{6,22},{7,23},{8,24},{9,... | collective-permute-start | bytes 393224 | tf_op jit(solution)/shard_map/ppermute | solution.py:58
  415.9 31.6 %collective-permute-start.8 = (f32[128,256]{1,0:T(8,128)S(1)}, f32[128,256]{1,0:T(8,128)S(1)}, u32[]{:S(2)}, u32[]{:S(2)}) collective-permute-start(f32[128,256]{1,0:T(8,128)S(1)} %select_add_fusion), channel_id=1, source_target_pairs={{0,1},{1,0},{2,3},{3,2},{4,5},{5,4},{6,7},{7,6},{8,9},{9,8},{10,11... | collective-permute-start | bytes 393224 | tf_op jit(solution)/shard_map/ppermute | solution.py:58
  447.5 46.7 %collective-permute-start.11 = (f32[128,256]{1,0:T(8,128)S(1)}, f32[128,256]{1,0:T(8,128)S(1)}, u32[]{:S(2)}, u32[]{:S(2)}) collective-permute-start(f32[128,256]{1,0:T(8,128)S(1)} %add_add_fusion), channel_id=1, source_target_pairs={{0,2},{1,3},{2,0},{3,1},{4,6},{5,7},{6,4},{7,5},{8,10},{9,11},{10,... | collective-permute-start | bytes 393224 | tf_op jit(solution)/shard_map/ppermute | solution.py:65
  494.2 38.9 %collective-permute-start.12 = (f32[128,256]{1,0:T(8,128)S(1)}, f32[128,256]{1,0:T(8,128)S(1)}, u32[]{:S(2)}, u32[]{:S(2)}) collective-permute-start(f32[128,256]{1,0:T(8,128)S(1)} %add.98), channel_id=1, source_target_pairs={{0,4},{1,5},{2,6},{3,7},{4,0},{5,1},{6,2},{7,3},{8,12},{9,13},{10,... | collective-permute-start | bytes 393224 | tf_op jit(solution)/shard_map/ppermute | solution.py:65
  533.1 52.1 %all-to-all-start.2 = ((f32[8,16,4,8,128]{4,3,2,1,0:T(8,128)}), f32[8,16,4,8,128]{4,3,2,1,0:T(8,128)S(1)}, u32[]{:S(2)}, u32[]{:S(2)}) async-start(f32[8,16,4,8,128]{4,3,2,1,0:T(8,128)} %copy_bitcast_fusion.2), calls=%async_computation.2 | async-start | bytes 4194304 | tf_op jit(solution)/shard_map/all_to_all | solution.py:459
  536.9 1.4 collective-permute-start.13
  591.6 1.4 collective-permute-start.14
  593.0 5.9 collective-permute-start.17
  595.5 5.5 collective-permute-start.16
  596.0 5.0 collective-permute-start.15
  601.0 4.7 collective-permute-start.18
  605.7 6.5 %collective-permute-start.19 = (f32[64,384]{1,0:T(8,128)S(1)}, f32[64,384]{1,0:T(8,128)S(1)}, u32[]{:S(2)}, u32[]{:S(2)}) collective-permute-start(f32[64,384]{1,0:T(8,128)S(1)} %add.111), channel_id=1, source_target_pairs={{0,4},{1,5},{2,6},{3,7},{4,0},{5,1},{6,2},{7,3},{8,12},{9,13},{10,... | collective-permute-start | bytes 294920 | tf_op jit(solution)/shard_map/ppermute | solution.py:65
  612.2 1.4 collective-permute-start.20
  (5 other events, 86.4 us)
